TPU v7x, 128 devices: a whole 4x4x4 slice. The times are simulated.
128 devices in a mesh: obs: 8 (over x, core), flux: 16 (over z, y).
Axes of the slice: x: 4, y: 4, z: 4, core: 2. Of those that a mesh axis runs over, the one named last changes fastest.
Arguments:
- probes: bfloat16 [768, 32, 128], P('flux'), may hold values from -6 to 6
- prior_tiles: bfloat16 [768, 8, 128, 128], P('flux'), may hold values from -0.1875 to 0.1875
- neighbours: int32 [768, 8], P('flux'), may hold values from 0 to 767, as said below
- jac: bfloat16 [8, 16, 384, 128, 128], P('obs', 'flux'), may hold values from -0.0390625 to 0.0390625
- jac_obs: int32 [8, 16, 384], P('obs', 'flux'), may hold values from 0 to 31
- jac_flux: int32 [8, 16, 384], P('obs', 'flux'), may hold values from 0 to 47
- counts: int32 [8, 16], P('obs', 'flux'), may hold values from 96 to 384
- rinv: float32 [256, 128], P('obs'), may hold values from 0.25 to 2.5
Outputs:
- power: bfloat16 [768, 32, 128], P('flux')
Inputs may be any that keep to these rules, and one draw needn't show every extreme that they name: `neighbours`: every entry lies within 12 tiles of its own tile t, and entry 0 is t itself.
All inputs are finite; a program needn't handle non-finite values.
Results may differ from a plain program's by a relative error of at most 0.024.
Values may be sent and summed in bfloat16 or wider, within the bound.
A program may use at most 128 MiB of HBM per device.

v0:
```python
import jax
import jax.numpy as jnp
from jax import lax
from jax.sharding import PartitionSpec as P

STEPS = 4


def with_halo(value, sides, width):
    for axis, dim in sides:
        count, length = (lax.axis_size(axis), value.shape[dim])
        up = [(i, (i + 1) % count) for i in range(count - 1)]
        down = [(j, i) for i, j in up]
        last = lax.slice_in_dim(value, length - width, length, axis=dim)
        first = lax.slice_in_dim(value, 0, width, axis=dim)
        before = lax.ppermute(last, axis, up)
        after = lax.ppermute(first, axis, down)
        value = jnp.concatenate([before, value, after], axis=dim)
    return value


def shifted(block, axis, distance):
    devices = range(lax.axis_size(axis))
    route = [(i - distance, i) for i in devices if i - distance in devices]
    return lax.ppermute(block, axis, route)


def spread_tiles(field, prior_tiles, local_nbr, reach_tiles):
    padded = with_halo(field, (("flux", 0),), reach_tiles)
    gathered = jnp.take(padded, local_nbr, axis=0)
    return jnp.einsum(
        "tkpc,tkcd->tpd", gathered, prior_tiles, preferred_element_type=jnp.float32
    ).astype(jnp.bfloat16)


def gather_tiles(adjoint, prior_tiles, local_nbr, reach_tiles):
    tile_count = adjoint.shape[0]
    probe_count = adjoint.shape[1]
    width = adjoint.shape[2]
    contrib = jnp.einsum("tpd,tkcd->tkpc", adjoint, prior_tiles, preferred_element_type=jnp.float32)
    contrib = contrib.reshape(-1, probe_count, width)
    extended = jax.ops.segment_sum(
        contrib, local_nbr.reshape(-1), num_segments=tile_count + 2 * reach_tiles
    )
    lower_rim = extended[:reach_tiles]
    upper_rim = extended[reach_tiles + tile_count :]
    from_below = shifted(upper_rim.astype(jnp.bfloat16), "flux", 1).astype(upper_rim.dtype)
    from_above = shifted(lower_rim.astype(jnp.bfloat16), "flux", -1).astype(lower_rim.dtype)
    inner = extended[reach_tiles : reach_tiles + tile_count]
    inner = inner.at[:reach_tiles].add(from_below)
    inner = inner.at[tile_count - reach_tiles :].add(from_above)
    return inner.astype(jnp.bfloat16)


def shards(probes, prior_tiles, neighbours, jac, jac_obs, jac_flux, counts, rinv):
    f32 = jnp.float32
    half = jnp.bfloat16
    tile_count = probes.shape[0]
    reach_tiles = tile_count // 4
    obs_rows = rinv.shape[0]
    blocks = jac[0, 0]
    block_obs = jac_obs[0, 0]
    block_flux = jac_flux[0, 0]
    block_count = blocks.shape[0]
    first_tile = lax.axis_index("flux") * tile_count
    local_nbr = neighbours - first_tile + reach_tiles
    live = (jnp.arange(block_count, dtype=jnp.int32) < counts[0, 0]).astype(f32)
    field = probes
    for step in range(STEPS):
        spread = spread_tiles(field, prior_tiles, local_nbr, reach_tiles)
        picked = jnp.take(spread, block_flux, axis=0)
        product = jnp.einsum("npc,nco->npo", picked, blocks, preferred_element_type=f32)
        product = product * live[:, None, None]
        partial_obs = jax.ops.segment_sum(product, block_obs, num_segments=obs_rows)
        total = lax.psum(partial_obs.astype(jnp.bfloat16), "flux").astype(jnp.float32)
        weighted = (total * rinv[:, None, :]).astype(half)
        picked_obs = jnp.take(weighted, block_obs, axis=0)
        backward = jnp.einsum("npo,nco->npc", picked_obs, blocks, preferred_element_type=f32)
        backward = backward * live[:, None, None]
        partial_cells = jax.ops.segment_sum(backward, block_flux, num_segments=tile_count)
        adjoint = (
            lax.psum(partial_cells.astype(jnp.bfloat16), "obs").astype(jnp.float32).astype(half)
        )
        field = gather_tiles(adjoint, prior_tiles, local_nbr, reach_tiles)
    return field


def solution(mesh):
    placed = (
        P("flux", None, None),
        P("flux", None, None, None),
        P("flux", None),
        P("obs", "flux", None, None, None),
        P("obs", "flux", None),
        P("obs", "flux", None),
        P("obs", "flux"),
        P("obs", None),
    )
    return jax.shard_map(
        shards, mesh=mesh, in_specs=placed, out_specs=P("flux", None, None), check_vma=False
    )
```

profile of v0, /device:TPU:1, one launch (start us, length us, event | category | flops | bytes accessed | tf_op | source)
XLA Modules:
  0.0 1304.2 jit_solution(4016002755542580364)
XLA Ops:
  7.5 4.0 collective-permute-start
  21.8 7.7 fusion.109
  32.1 8.5 broadcast_multiply_fusion.7
  40.8 34.7 %scatter_fusion = f32[32,32,128]{2,1,0:T(8,128)S(1)} fusion(f32[32,32,128]{2,1,0:T(8,128)S(1)} %broadcast.129.clone.2, s32[384]{0:T(512)} %copy-done.10, f32[384,32,128]{2,1,0:T(8,128)} %broadcast_multiply_fusion.7), kind=kCustom, calls=%fused_computation.12 | custom fusion | flops 1572864 | bytes 18875904 | tf_op jit(solution)/shard_map/scatter-add | solution.py:74
  76.3 87.8 %all-reduce.9.cloned.1.call-done = bf16[32,32,128]{2,1,0:T(8,128)(2,1)} async-done(((bf16[32,32,128]{2,1,0:T(8,128)(2,1)}), bf16[32,32,128]{2,1,0:T(8,128)(2,1)}) %all-reduce.9.cloned.1.call-update) | async-done | bytes 262160 | tf_op jit(solution)/shard_map/psum | solution.py:75
  167.5 12.2 broadcast_multiply_fusion.6
  179.9 34.3 %scatter_fusion.1 = f32[48,32,128]{2,1,0:T(8,128)S(1)} fusion(f32[48,32,128]{2,1,0:T(8,128)S(1)} %broadcast.128.clone.2, s32[384]{0:T(512)S(1)} %copy-done.6, f32[384,32,128]{2,1,0:T(8,128)} %broadcast_multiply_fusion.6), kind=kCustom, calls=%fused_computation.13 | custom fusion | flops 1572864 | bytes 18875904 | tf_op jit(solution)/shard_map/scatter-add | solution.py:80
  215.5 59.5 %all-reduce.11.cloned.1.call-done = bf16[48,32,128]{2,1,0:T(8,128)(2,1)} async-done(((bf16[48,32,128]{2,1,0:T(8,128)(2,1)}), bf16[48,32,128]{2,1,0:T(8,128)(2,1)}) %all-reduce.11.cloned.1.call-update) | async-done | bytes 393232 | tf_op jit(solution)/shard_map/psum | solution.py:82
  275.0 11.8 fusion.118
  286.9 34.4 %scatter_fusion.2 = f32[72,32,128]{2,1,0:T(8,128)S(1)} fusion(f32[72,32,128]{2,1,0:T(8,128)S(1)} %broadcast.127.clone.2, s32[384]{0:T(512)S(1)} %reshape.451, f32[384,32,128]{2,1,0:T(8,128)} %bitcast.100), kind=kCustom, calls=%fused_computation.14 | custom fusion | flops 1572864 | bytes 18875904 | tf_op jit(solution)/shard_map/scatter-add | solution.py:42
  326.3 3.8 collective-permute-done.3
  330.2 3.4 collective-permute-start.4
  335.2 3.7 collective-permute-done.5
  339.0 3.1 gather_fusion.3
  342.2 7.7 fusion.106
  352.5 8.5 broadcast_multiply_fusion.5
  361.1 34.5 %scatter_fusion.3 = f32[32,32,128]{2,1,0:T(8,128)S(1)} fusion(f32[32,32,128]{2,1,0:T(8,128)S(1)} %broadcast.129.clone.1, s32[384]{0:T(512)} %copy-done.10, f32[384,32,128]{2,1,0:T(8,128)} %broadcast_multiply_fusion.5), kind=kCustom, calls=%fused_computation.15 | custom fusion | flops 1572864 | bytes 18875904 | tf_op jit(solution)/shard_map/scatter-add | solution.py:74
  396.8 89.1 %all-reduce.13.cloned.1.call-done = bf16[32,32,128]{2,1,0:T(8,128)(2,1)} async-done(((bf16[32,32,128]{2,1,0:T(8,128)(2,1)}), bf16[32,32,128]{2,1,0:T(8,128)(2,1)}) %all-reduce.13.cloned.1.call-update) | async-done | bytes 262160 | tf_op jit(solution)/shard_map/psum | solution.py:75
  489.4 12.2 broadcast_multiply_fusion.4
  501.8 34.3 %scatter_fusion.4 = f32[48,32,128]{2,1,0:T(8,128)S(1)} fusion(f32[48,32,128]{2,1,0:T(8,128)S(1)} %broadcast.128.clone.1, s32[384]{0:T(512)S(1)} %copy-done.7, f32[384,32,128]{2,1,0:T(8,128)} %broadcast_multiply_fusion.4), kind=kCustom, calls=%fused_computation.16 | custom fusion | flops 1572864 | bytes 18875904 | tf_op jit(solution)/shard_map/scatter-add | solution.py:80
  537.0 59.9 %all-reduce.15.cloned.1.call-done = bf16[48,32,128]{2,1,0:T(8,128)(2,1)} async-done(((bf16[48,32,128]{2,1,0:T(8,128)(2,1)}), bf16[48,32,128]{2,1,0:T(8,128)(2,1)}) %all-reduce.15.cloned.1.call-update) | async-done | bytes 393232 | tf_op jit(solution)/shard_map/psum | solution.py:82
  596.9 11.8 fusion.116
  608.8 34.4 %scatter_fusion.5 = f32[72,32,128]{2,1,0:T(8,128)S(1)} fusion(f32[72,32,128]{2,1,0:T(8,128)S(1)} %broadcast.127.clone.1, s32[384]{0:T(512)S(1)} %copy-done.14, f32[384,32,128]{2,1,0:T(8,128)} %bitcast.101), kind=kCustom, calls=%fused_computation.17 | custom fusion | flops 1572864 | bytes 18875904 | tf_op jit(solution)/shard_map/scatter-add | solution.py:42
  648.1 3.8 collective-permute-done.7
  652.1 3.4 collective-permute-start.8
  657.1 3.7 collective-permute-done.9
  664.1 7.7 fusion.103
  674.3 8.5 broadcast_multiply_fusion.3
  683.0 34.5 %scatter_fusion.6 = f32[32,32,128]{2,1,0:T(8,128)S(1)} fusion(f32[32,32,128]{2,1,0:T(8,128)S(1)} %broadcast.129.clone, s32[384]{0:T(512)} %copy-done.10, f32[384,32,128]{2,1,0:T(8,128)} %broadcast_multiply_fusion.3), kind=kCustom, calls=%fused_computation.18 | custom fusion | flops 1572864 | bytes 18875904 | tf_op jit(solution)/shard_map/scatter-add | solution.py:74
  718.3 89.5 %all-reduce.17.cloned.1.call-done = bf16[32,32,128]{2,1,0:T(8,128)(2,1)} async-done(((bf16[32,32,128]{2,1,0:T(8,128)(2,1)}), bf16[32,32,128]{2,1,0:T(8,128)(2,1)}) %all-reduce.17.cloned.1.call-update) | async-done | bytes 262160 | tf_op jit(solution)/shard_map/psum | solution.py:75
  811.3 12.2 broadcast_multiply_fusion.2
  823.6 34.3 %scatter_fusion.7 = f32[48,32,128]{2,1,0:T(8,128)S(1)} fusion(f32[48,32,128]{2,1,0:T(8,128)S(1)} %broadcast.128.clone, s32[384]{0:T(512)S(1)} %copy-done.8, f32[384,32,128]{2,1,0:T(8,128)} %broadcast_multiply_fusion.2), kind=kCustom, calls=%fused_computation.19 | custom fusion | flops 1572864 | bytes 18875904 | tf_op jit(solution)/shard_map/scatter-add | solution.py:80
  859.1 59.7 %all-reduce.19.cloned.1.call-done = bf16[48,32,128]{2,1,0:T(8,128)(2,1)} async-done(((bf16[48,32,128]{2,1,0:T(8,128)(2,1)}), bf16[48,32,128]{2,1,0:T(8,128)(2,1)}) %all-reduce.19.cloned.1.call-update) | async-done | bytes 393232 | tf_op jit(solution)/shard_map/psum | solution.py:82
  918.8 11.8 fusion.114
  930.7 34.4 %scatter_fusion.8 = f32[72,32,128]{2,1,0:T(8,128)S(1)} fusion(f32[72,32,128]{2,1,0:T(8,128)S(1)} %broadcast.127.clone, s32[384]{0:T(512)S(1)} %copy-done.15, f32[384,32,128]{2,1,0:T(8,128)} %bitcast.102), kind=kCustom, calls=%fused_computation.20 | custom fusion | flops 1572864 | bytes 18875904 | tf_op jit(solution)/shard_map/scatter-add | solution.py:42
  970.0 3.8 collective-permute-done.11
  974.0 3.4 collective-permute-start.12
  979.0 3.7 collective-permute-done.13
  985.9 7.7 fusion.100
  996.3 9.1 broadcast_multiply_fusion.1
  1005.4 34.4 %scatter_fusion.9 = f32[32,32,128]{2,1,0:T(8,128)S(1)} fusion(f32[32,32,128]{2,1,0:T(8,128)S(1)} %broadcast.129, s32[384]{0:T(512)S(1)} %copy-done.12, f32[384,32,128]{2,1,0:T(8,128)} %broadcast_multiply_fusion.1), kind=kCustom, calls=%fused_computation.21 | custom fusion | flops 1572864 | bytes 18875904 | tf_op jit(solution)/shard_map/scatter-add | solution.py:74
  1040.9 89.2 %all-reduce.21.cloned.1.call-done = bf16[32,32,128]{2,1,0:T(8,128)(2,1)} async-done(((bf16[32,32,128]{2,1,0:T(8,128)(2,1)}), bf16[32,32,128]{2,1,0:T(8,128)(2,1)}) %all-reduce.21.cloned.1.call-update) | async-done | bytes 262160 | tf_op jit(solution)/shard_map/psum | solution.py:75
  1133.6 12.2 broadcast_multiply_fusion
  1145.9 34.3 %scatter_fusion.10 = f32[48,32,128]{2,1,0:T(8,128)S(1)} fusion(f32[48,32,128]{2,1,0:T(8,128)S(1)} %broadcast.128, s32[384]{0:T(512)S(1)} %copy-done.9, f32[384,32,128]{2,1,0:T(8,128)} %broadcast_multiply_fusion), kind=kCustom, calls=%fused_computation.22 | custom fusion | flops 1572864 | bytes 18875904 | tf_op jit(solution)/shard_map/scatter-add | solution.py:80
  1181.1 59.9 %all-reduce.23.cloned.1.call-done = bf16[48,32,128]{2,1,0:T(8,128)(2,1)} async-done(((bf16[48,32,128]{2,1,0:T(8,128)(2,1)}), bf16[48,32,128]{2,1,0:T(8,128)(2,1)}) %all-reduce.23.cloned.1.call-update) | async-done | bytes 393232 | tf_op jit(solution)/shard_map/psum | solution.py:82
  1241.1 11.8 fusion.112
  1253.0 34.4 %scatter_fusion.11 = f32[72,32,128]{2,1,0:T(8,128)S(1)} fusion(f32[72,32,128]{2,1,0:T(8,128)S(1)} %broadcast.127, s32[384]{0:T(512)S(1)} %copy-done.16, f32[384,32,128]{2,1,0:T(8,128)} %bitcast.99), kind=kCustom, calls=%fused_computation.23 | custom fusion | flops 1572864 | bytes 18875904 | tf_op jit(solution)/shard_map/scatter-add | solution.py:42
  1292.3 3.8 collective-permute-done.15
  (174 shorter events, 75.5 us)
Async XLA Ops:
  6.5 157.5 %all-reduce.9.cloned.1.call-start = ((), (), s32[]{:S(2)}) async-start(), calls=%async_computation | async-start | bytes 524288 | tf_op jit(solution)/shard_map/psum | solution.py:75
  7.5 10.1 collective-permute-start
  11.5 6.1 collective-permute-start.1
  14.5 3.1 copy-start.5
  40.7 35.5 %copy-start.26 = (s32[384]{0:T(512)S(1)}, s32[384]{0:T(512)}, u32[]{:S(2)}) copy-start(s32[384]{0:T(512)} %compare_select_fusion.1) | copy-start | bytes 4612
  40.7 35.5 %copy-start.11 = (s32[384]{0:T(512)S(1)}, s32[384]{0:T(512)}, u32[]{:S(2)}) copy-start(s32[384]{0:T(512)} %copy-done.10) | copy-start | bytes 4612
  40.7 123.3 %copy-start = (f32[32,128]{1,0:T(8,128)S(1)}, f32[32,128]{1,0:T(8,128)}, u32[]{:S(2)}) copy-start(f32[32,128]{1,0:T(8,128)} %param.37) | copy-start | bytes 49156
  76.2 198.8 %all-reduce.11.cloned.1.call-start = ((), (), s32[]{:S(2)}) async-start(), calls=%async_computation.1 | async-start | bytes 786432 | tf_op jit(solution)/shard_map/psum | solution.py:82
  76.3 88.8 %copy-start.17 = (s32[1024]{0:T(1024)}, s32[1024]{0:T(1024)S(1)}, u32[]{:S(2)}) copy-start(s32[1024]{0:T(1024)S(1)} %pad_clamp_fusion) | copy-start | bytes 12292
  76.3 91.2 %copy-start.22 = (pred[384]{0:T(512)(128)(4,1)}, pred[384]{0:T(512)(128)(4,1)S(1)}, u32[]{:S(2)}) copy-start(pred[384]{0:T(512)(128)(4,1)S(1)} %compare_and_fusion.1) | copy-start | bytes 1156
  167.5 12.3 copy-start.6
  179.9 35.5 %copy-start.21 = (s32[48,8]{0,1:T(8,128)S(1)}, s32[48,8]{0,1:T(8,128)}, u32[]{:S(2)}) copy-start(s32[48,8]{0,1:T(8,128)} %param.32) | copy-start | bytes 4612
  215.1 270.9 %all-reduce.13.cloned.1.call-start = ((), (), s32[]{:S(2)}) async-start(), calls=%async_computation.2 | async-start | bytes 524288 | tf_op jit(solution)/shard_map/psum | solution.py:75
  215.5 71.4 %copy-start.13 = (s32[384]{0:T(512)}, s32[384]{0:T(512)S(1)}, u32[]{:S(2)}) copy-start(s32[384]{0:T(512)S(1)} %reshape.451) | copy-start | bytes 4612
  321.5 4.7 collective-permute-start.2
  324.7 5.4 collective-permute-start.3
  330.2 5.0 collective-permute-start.4
  333.6 5.4 collective-permute-start.5
  361.1 124.9 %copy-start.1 = (f32[32,128]{1,0:T(8,128)S(1)}, f32[32,128]{1,0:T(8,128)}, u32[]{:S(2)}) copy-start(f32[32,128]{1,0:T(8,128)} %param.37) | copy-start | bytes 49156
  361.1 125.9 %copy-start.18 = (s32[1024]{0:T(1024)S(1)}, s32[1024]{0:T(1024)}, u32[]{:S(2)}) copy-start(s32[1024]{0:T(1024)} %copy-done.17) | copy-start | bytes 12292
  396.4 200.5 %all-reduce.15.cloned.1.call-start = ((), (), s32[]{:S(2)}) async-start(), calls=%async_computation.3 | async-start | bytes 786432 | tf_op jit(solution)/shard_map/psum | solution.py:82
  487.0 2.5 copy-start.23
  489.4 12.3 copy-start.7
  537.0 71.9 %copy-start.14 = (s32[384]{0:T(512)S(1)}, s32[384]{0:T(512)}, u32[]{:S(2)}) copy-start(s32[384]{0:T(512)} %copy-done.13) | copy-start | bytes 4612
  537.0 270.9 %all-reduce.17.cloned.1.call-start = ((), (), s32[]{:S(2)}) async-start(), calls=%async_computation.4 | async-start | bytes 524288 | tf_op jit(solution)/shard_map/psum | solution.py:75
  643.4 4.7 collective-permute-start.6
  646.6 5.4 collective-permute-start.7
  652.1 5.0 collective-permute-start.8
  655.5 5.4 collective-permute-start.9
  683.0 124.9 %copy-start.2 = (f32[32,128]{1,0:T(8,128)S(1)}, f32[32,128]{1,0:T(8,128)}, u32[]{:S(2)}) copy-start(f32[32,128]{1,0:T(8,128)} %param.37) | copy-start | bytes 49156
  683.0 125.9 %copy-start.19 = (s32[1024]{0:T(1024)S(1)}, s32[1024]{0:T(1024)}, u32[]{:S(2)}) copy-start(s32[1024]{0:T(1024)} %copy-done.17) | copy-start | bytes 12292
  718.3 200.5 %all-reduce.19.cloned.1.call-start = ((), (), s32[]{:S(2)}) async-start(), calls=%async_computation.5 | async-start | bytes 786432 | tf_op jit(solution)/shard_map/psum | solution.py:82
  811.3 12.3 copy-start.8
  858.8 71.9 %copy-start.15 = (s32[384]{0:T(512)S(1)}, s32[384]{0:T(512)}, u32[]{:S(2)}) copy-start(s32[384]{0:T(512)} %copy-done.13) | copy-start | bytes 4612
  858.8 271.3 %all-reduce.21.cloned.1.call-start = ((), (), s32[]{:S(2)}) async-start(), calls=%async_computation.6 | async-start | bytes 524288 | tf_op jit(solution)/shard_map/psum | solution.py:75
  965.3 4.7 collective-permute-start.10
  968.4 5.4 collective-permute-start.11
  974.0 5.0 collective-permute-start.12
  977.4 5.4 collective-permute-start.13
  993.7 2.6 copy-start.4
  996.2 9.1 copy-start.12
  1005.4 124.7 %copy-start.3 = (f32[32,128]{1,0:T(8,128)S(1)}, f32[32,128]{1,0:T(8,128)}, u32[]{:S(2)}) copy-start(f32[32,128]{1,0:T(8,128)} %param.37) | copy-start | bytes 49156
  1005.4 125.7 %copy-start.20 = (s32[1024]{0:T(1024)S(1)}, s32[1024]{0:T(1024)}, u32[]{:S(2)}) copy-start(s32[1024]{0:T(1024)} %copy-done.17) | copy-start | bytes 12292
  1040.6 200.5 %all-reduce.23.cloned.1.call-start = ((), (), s32[]{:S(2)}) async-start(), calls=%async_computation.7 | async-start | bytes 786432 | tf_op jit(solution)/shard_map/psum | solution.py:82
  1133.6 12.3 copy-start.9
  1181.1 71.9 %copy-start.16 = (s32[384]{0:T(512)S(1)}, s32[384]{0:T(512)}, u32[]{:S(2)}) copy-start(s32[384]{0:T(512)} %copy-done.13) | copy-start | bytes 4612
  1287.6 4.7 collective-permute-start.14
  1290.7 5.4 collective-permute-start.15
  (3 other events, 6.1 us)
Sparse Core Ops, SparseCore 0:
  76.3 87.7 all-reduce.8
  215.2 59.7 all-reduce.10
  396.5 89.3 all-reduce.12
  537.1 59.7 all-reduce.14
  718.4 89.3 all-reduce.16
  859.0 59.7 all-reduce.18
  1040.7 89.3 all-reduce.20
  1181.2 59.7 all-reduce.22
where the time goes:
time: 1330 us; the launch traced here: 1300 us
  waiting for transfers between devices  623 us (47%)
  other arithmetic  430 us (32%)
  matrix products  162 us (12%)
  starting transfers between devices  38.4 us (3%)
  local copies, waits for them, and re-layouts  35.4 us (3%)
  between operations  15.6 us (1%)
    psum x4, waiting for transfers between devices, shards(): lax.psum(partial_obs.astype(jnp.bfloat16), 'flux').astype(jnp.float32)  356 us
    psum x4, waiting for transfers between devices, shards(): lax.psum(partial_cells.astype(jnp.bfloat16), 'obs').astype(jnp.float32)  239 us
    scatter-add x4, other arithmetic, shards(): partial_obs = jax.ops.segment_sum(product, block_obs, num_segments=obs_rows)  138 us
    scatter-add x4, other arithmetic, gather_tiles(): jax.ops.segment_sum(contrib, local_nbr.reshape(-1), num_segments=tile_cou...  138 us
    scatter-add x4, other arithmetic, shards(): jax.ops.segment_sum(backward, block_flux, num_segments=tile_count)  137 us
    dot_general x4, matrix products, shards(): jnp.einsum('npo,nco->npc', picked_obs, blocks, preferred_element_type=f32)  48.9 us
    dot_general x4, matrix products, gather_tiles(): jnp.einsum('tpd,tkcd->tkpc', adjoint, prior_tiles, preferred_element_type...  47.2 us
    dot_general x4, matrix products, shards(): jnp.einsum('npc,nco->npo', picked, blocks, preferred_element_type=f32)  34.7 us
  transfers between devices with their start and end apart: 24, of which 22 were waited for; matrix products, arithmetic and copies ran while one was open for 0% of the time, Pallas kernels for 0%

commit v1 on v0

v1 whole, which is shorter than its diff:
```python
import functools

import jax
import jax.numpy as jnp
from jax import lax
from jax.experimental import pallas as pl
from jax.experimental.pallas import tpu as pltpu
from jax.sharding import PartitionSpec as P

STEPS = 4
REACH = 12
SIDE = 2
MESH = pl.DeviceIdType.MESH
F32 = jnp.float32
BF16 = jnp.bfloat16


def segment_pairs(key, lhs, segments, zero_lhs, pairs):
    count = key.shape[0]
    order = jnp.arange(count, dtype=jnp.int32)
    names = jnp.arange(segments, dtype=jnp.int32)
    hot = (key[:, None] == names[None, :]).astype(jnp.int32)
    size = jnp.sum(hot, axis=0)
    even = (size + 1) // 2 * 2
    begin = jnp.sum(jnp.where(names[None, :] < names[:, None], even[None, :], 0), axis=1)
    same = (key[None, :] == key[:, None]) & (order[None, :] < order[:, None])
    rank = jnp.sum(same.astype(jnp.int32), axis=1)
    place = jnp.where(key < segments, jnp.sum(hot * begin[None, :], axis=1) + rank, -1)
    slots = jnp.arange(2 * pairs, dtype=jnp.int32)
    match = slots[:, None] == place[None, :]
    block = jnp.sum(jnp.where(match, order[None, :], 0), axis=1)
    left = zero_lhs + jnp.sum(jnp.where(match, lhs[None, :] - zero_lhs, 0), axis=1)
    opens = (slots[::2][:, None] == begin[None, :]) & (size > 0)[None, :]
    flag = 1 - jnp.sum(opens.astype(jnp.int32), axis=1)
    last = jnp.where(size > 0, (begin + even) // 2 - 1, pairs)
    return jnp.concatenate([block, left, flag, last]).astype(jnp.int32)


def unroll_of(total, most):
    return max(u for u in range(1, most + 1) if total % u == 0)


def kernel(
    g, idx, probes, prior, jac, rinv, out,
    blocks, flipped, prior_own, prior_flip, ext, spread, weighted, adjoint, scan,
    part_obs, got_obs, part_cell, got_cell, part_field, got_field,
    load_sem, fs, fr, ws, wr, os_, or_, gs, gr, cs, cr, es, er,
):
    no, nf, chunk = g["no"], g["nf"], g["chunk"]
    tiles, obs_blocks, nbrs, slots = g["tiles"], g["obs_blocks"], g["nbrs"], g["slots"]
    mine = obs_blocks // nf
    reach = (2 * SIDE + 1) * chunk
    o = lax.axis_index("obs")
    f = lax.axis_index("flux")
    chunks = no * nf

    def chunk_of(o_, f_):
        odd = lax.rem(f_, 2)
        return odd * (no - 1 - o_) + (1 - odd) * o_

    c = chunk_of(o, f)
    q = f * no + c

    def holder(distance):
        at = lax.rem(q + distance + chunks, chunks)
        f_ = lax.div(at, no)
        return (chunk_of(lax.rem(at, no), f_), f_)

    def flux_peer(r):
        return (o, lax.rem(f + r, nf))

    def obs_peer(r):
        return (lax.rem(o + r, no), f)

    sides = [d for d in range(-SIDE, SIDE + 1) if d != 0]

    load_jac = pltpu.make_async_copy(jac, blocks, load_sem.at[0])
    load_prior = pltpu.make_async_copy(prior.at[pl.ds(c * chunk, chunk)], prior_own, load_sem.at[1])
    load_field = pltpu.make_async_copy(
        probes.at[pl.ds(c * chunk, chunk)], ext.at[pl.ds(SIDE * chunk, chunk)], load_sem.at[2]
    )
    load_field.start()
    load_prior.start()
    load_jac.start()

    barrier = pltpu.get_barrier_semaphore()
    partners = [flux_peer(r) for r in range(1, nf)] + [obs_peer(r) for r in range(1, no)]
    partners += [holder(d) for d in sides]
    for partner in partners:
        pl.semaphore_signal(barrier, inc=1, device_id=partner, device_id_type=MESH)
    pl.semaphore_wait(barrier, len(partners))

    zero = jnp.zeros(spread.shape[1:], BF16)
    spread[tiles] = zero
    weighted[obs_blocks] = zero
    adjoint[chunk] = zero

    def remote(src, dst, send, recv, device):
        return pltpu.make_async_remote_copy(
            src_ref=src, dst_ref=dst, send_sem=send, recv_sem=recv, device_id=device, device_id_type=MESH
        )

    def start_all(copies):
        for copy in copies:
            copy.start()

    def wait_all(copies):
        for copy in copies:
            copy.wait_recv()
        for copy in copies:
            copy.wait_send()

    def products(base, pairs, lhs_ref, rhs_ref, unroll):
        def one(m, acc):
            a, b = base + 2 * m, base + 2 * m + 1
            left = jnp.concatenate([lhs_ref[idx[2 * pairs + a]], lhs_ref[idx[2 * pairs + b]]], axis=1)
            right = jnp.concatenate([rhs_ref[idx[a]], rhs_ref[idx[b]]], axis=0)
            acc = acc * idx[base + 4 * pairs + m].astype(F32)
            acc = acc + jnp.dot(left, right, preferred_element_type=F32)
            scan[m] = acc
            return acc

        def some(i, acc):
            for u in range(unroll):
                acc = one(i * unroll + u, acc)
            return acc

        lax.fori_loop(0, pairs // unroll, some, jnp.zeros(scan.shape[1:], F32))
        scan[pairs] = jnp.zeros(scan.shape[1:], F32)
        return base + 5 * pairs

    def field_copies():
        own = ext.at[pl.ds(SIDE * chunk, chunk)]
        return [
            remote(own, ext.at[pl.ds((SIDE - d) * chunk, chunk)], es.at[i], er.at[i], holder(d))
            for i, d in enumerate(sides)
        ]

    def gather_copies():
        own = spread.at[pl.ds(c * chunk, chunk)]
        return [remote(own, own, gs.at[r - 1], gr.at[r - 1], obs_peer(r)) for r in range(1, no)]

    load_field.wait()

    def step(s, carry):
        copies = field_copies()
        start_all(copies)

        @pl.when(s == 0)
        def _():
            load_prior.wait()

        wait_all(copies)

        def spread_one(t, carry):
            left = jnp.concatenate([ext[idx[g["nbr_at"] + t * nbrs + k]] for k in range(nbrs)], axis=1)
            right = prior_own[t].reshape(nbrs * prior_own.shape[2], prior_own.shape[3])
            spread[c * chunk + t] = jnp.dot(left, right, preferred_element_type=F32).astype(BF16)
            return carry

        for t in range(chunk):
            spread_one(t, 0)
        copies = gather_copies()
        start_all(copies)

        @pl.when(s == 0)
        def _():
            load_jac.wait()

            def flip(e, carry):
                t, k = e // nbrs, e % nbrs
                prior_flip[e] = prior_own[t, k].T
                return carry

            for e in range(chunk * nbrs):
                flip(e, 0)

        wait_all(copies)

        last = products(g["fwd_at"], g["fwd_pairs"], spread, blocks, g["fwd_unroll"])
        for b in range(obs_blocks):
            part_obs[b] = scan[idx[last + b]].astype(BF16)
        copies = []
        for r in range(1, nf):
            peer = flux_peer(r)
            copies.append(
                remote(part_obs.at[pl.ds(peer[1] * mine, mine)], got_obs.at[r - 1], fs.at[r - 1], fr.at[r - 1], peer)
            )
        start_all(copies)

        @pl.when(s == 0)
        def _():
            many = unroll_of(slots, 8)

            def flip(i, carry):
                for u in range(many):
                    flipped[i * many + u] = blocks[i * many + u].T
                return carry

            lax.fori_loop(0, slots // many, flip, 0)

        wait_all(copies)
        for b in range(mine):
            total = scan[idx[last + f * mine + b]]
            for r in range(1, nf):
                total = total + got_obs[r - 1, b].astype(F32)
            weighted[f * mine + b] = (total * rinv[pl.ds(f * mine + b, 1), :]).astype(BF16)
        own = weighted.at[pl.ds(f * mine, mine)]
        copies = [remote(own, own, ws.at[r - 1], wr.at[r - 1], flux_peer(r)) for r in range(1, nf)]
        start_all(copies)
        wait_all(copies)

        last = products(g["adj_at"], g["adj_pairs"], weighted, flipped, g["adj_unroll"])
        for t in range(tiles):
            part_cell[t] = scan[idx[last + t]].astype(BF16)
        copies = []
        for r in range(1, no):
            peer = obs_peer(r)
            at = chunk_of(peer[0], f) * chunk
            copies.append(
                remote(part_cell.at[pl.ds(at, chunk)], got_cell.at[r - 1], os_.at[r - 1], or_.at[r - 1], peer)
            )
        start_all(copies)
        wait_all(copies)
        for t in range(chunk):
            total = scan[idx[last + c * chunk + t]]
            for r in range(1, no):
                total = total + got_cell[r - 1, t].astype(F32)
            adjoint[t] = total.astype(BF16)

        last = products(g["gat_at"], g["gat_pairs"], adjoint, prior_flip, g["gat_unroll"])
        for j in range(reach):
            if j // chunk != SIDE:
                part_field[j] = scan[idx[last + j]].astype(BF16)
        copies = [
            remote(part_field.at[pl.ds((SIDE + d) * chunk, chunk)], got_field.at[i], cs.at[i], cr.at[i], holder(d))
            for i, d in enumerate(sides)
        ]
        start_all(copies)
        wait_all(copies)
        for t in range(chunk):
            total = scan[idx[last + SIDE * chunk + t]]
            for i in range(len(sides)):
                total = total + got_field[i, t].astype(F32)
            ext[SIDE * chunk + t] = total.astype(BF16)
        return carry

    lax.fori_loop(0, STEPS, step, 0)
    for t in range(chunk):
        spread[c * chunk + t] = ext[SIDE * chunk + t]
    copies = gather_copies()
    start_all(copies)
    wait_all(copies)
    out[...] = spread[pl.ds(0, tiles)]


def shards(no, nf, probes, prior_tiles, neighbours, jac, jac_obs, jac_flux, counts, rinv):
    tiles, probe_count, width = probes.shape
    nbrs = prior_tiles.shape[1]
    obs_blocks = rinv.shape[0]
    slots = jac.shape[2]
    chunk = tiles // no
    assert SIDE * chunk == REACH and obs_blocks % nf == 0
    reach = (2 * SIDE + 1) * chunk
    fwd_pairs = (slots + obs_blocks) // 2
    adj_pairs = (slots + tiles) // 2
    gat_pairs = (chunk * nbrs + reach) // 2
    o = lax.axis_index("obs")
    f = lax.axis_index("flux")
    c = jnp.where(f % 2 == 1, no - 1 - o, o)
    live = jnp.arange(slots, dtype=jnp.int32) < counts[0, 0]
    block_obs, block_flux = jac_obs[0, 0], jac_flux[0, 0]
    own = lax.dynamic_slice_in_dim(neighbours, c * chunk, chunk, 0).reshape(-1)
    own = own - (f * tiles + c * chunk - SIDE * chunk)
    entry_tile = jnp.arange(chunk * nbrs, dtype=jnp.int32) // nbrs
    fwd = segment_pairs(jnp.where(live, block_obs, obs_blocks), block_flux, obs_blocks, tiles, fwd_pairs)
    adj = segment_pairs(jnp.where(live, block_flux, tiles), block_obs, tiles, obs_blocks, adj_pairs)
    gat = segment_pairs(own, entry_tile, reach, chunk, gat_pairs)
    idx = jnp.concatenate([fwd, adj, gat, own])
    g = dict(
        no=no, nf=nf, chunk=chunk, tiles=tiles, obs_blocks=obs_blocks, nbrs=nbrs, slots=slots,
        fwd_pairs=fwd_pairs, adj_pairs=adj_pairs, gat_pairs=gat_pairs,
        fwd_at=0, adj_at=fwd.shape[0], gat_at=fwd.shape[0] + adj.shape[0],
        nbr_at=fwd.shape[0] + adj.shape[0] + gat.shape[0],
        fwd_unroll=unroll_of(fwd_pairs, 56), adj_unroll=unroll_of(adj_pairs, 56),
        gat_unroll=unroll_of(gat_pairs, 56),
    )
    mine = obs_blocks // nf
    tile = (probe_count, width)
    dma = pltpu.SemaphoreType.DMA
    most = max(fwd_pairs, adj_pairs, gat_pairs) + 1
    vmem = pl.BlockSpec(memory_space=pltpu.VMEM)
    any_space = pl.BlockSpec(memory_space=pl.ANY)
    return pl.pallas_call(
        functools.partial(kernel, g),
        out_shape=jax.ShapeDtypeStruct((tiles,) + tile, BF16),
        in_specs=[pl.BlockSpec(memory_space=pltpu.SMEM), any_space, any_space, any_space, vmem],
        out_specs=vmem,
        scratch_shapes=[
            pltpu.VMEM((slots, width, width), BF16),
            pltpu.VMEM((slots, width, width), BF16),
            pltpu.VMEM((chunk, nbrs, width, width), BF16),
            pltpu.VMEM((chunk * nbrs, width, width), BF16),
            pltpu.VMEM((reach,) + tile, BF16),
            pltpu.VMEM((tiles + 1,) + tile, BF16),
            pltpu.VMEM((obs_blocks + 1,) + tile, BF16),
            pltpu.VMEM((chunk + 1,) + tile, BF16),
            pltpu.VMEM((most,) + tile, F32),
            pltpu.VMEM((obs_blocks,) + tile, BF16),
            pltpu.VMEM((nf - 1, mine) + tile, BF16),
            pltpu.VMEM((tiles,) + tile, BF16),
            pltpu.VMEM((no - 1, chunk) + tile, BF16),
            pltpu.VMEM((reach,) + tile, BF16),
            pltpu.VMEM((2 * SIDE, chunk) + tile, BF16),
            dma((3,)),
            dma((nf - 1,)), dma((nf - 1,)), dma((nf - 1,)), dma((nf - 1,)),
            dma((no - 1,)), dma((no - 1,)), dma((no - 1,)), dma((no - 1,)),
            dma((2 * SIDE,)), dma((2 * SIDE,)), dma((2 * SIDE,)), dma((2 * SIDE,)),
        ],
        compiler_params=pltpu.CompilerParams(
            collective_id=0, has_side_effects=True, vmem_limit_bytes=48 * 1024 * 1024
        ),
    )(idx, probes, prior_tiles, jac[0, 0], rinv)


def solution(mesh):
    placed = (
        P("flux", None, None),
        P("flux", None, None, None),
        P("flux", None),
        P("obs", "flux", None, None, None),
        P("obs", "flux", None),
        P("obs", "flux", None),
        P("obs", "flux"),
        P("obs", None),
    )
    return jax.shard_map(
        functools.partial(shards, mesh.shape["obs"], mesh.shape["flux"]),
        mesh=mesh, in_specs=placed, out_specs=P("flux", None, None), check_vma=False,
    )
```

time: 1330 us -> 183 us (0.14); the launches traced: 1300 us -> 183 us
  waiting for transfers between devices: 623 us -> 0 us
  other arithmetic: 430 us -> 4.91 us
  Pallas kernels: 0 us -> 174 us
  matrix products: 162 us -> 0 us
  starting transfers between devices: 38.4 us -> 0 us
  local copies, waits for them, and re-layouts: 35.4 us -> 3.29 us
  between operations: 15.6 us -> 0.8 us
    psum x8 -> x0, waiting for transfers between devices: 595 us -> none  [the longest x4 356 us: shards(): lax.psum(partial_obs.astype(jnp.bfloat16), 'flux').astype(jnp.float32)]
    scatter-add x20 -> x0, other arithmetic: 413 us -> none  [the longest x4 138 us: shards(): partial_obs = jax.ops.segment_sum(product, block_obs, num_segments=obs_rows)]
    pallas_call x0 -> x1, Pallas kernels: none -> 174 us  [shards(): pl.pallas_call(functools.partial(kernel, g), out_shape=jax.ShapeDtypeStru...]
    dot_general x16 -> x0, matrix products: 162 us -> none  [the longest x4 48.9 us: shards(): jnp.einsum('npo,nco->npc', picked_obs, blocks, preferred_element_type=f32)]
    ppermute x16 -> x0, starting transfers between devices: 37.1 us -> none  [the longest x8 17.5 us: shifted(): return lax.ppermute(block, axis, route)]
    gather x12 -> x0, local copies, waits for them, and re-layouts: 32.6 us -> none  [the longest x4 12.5 us: spread_tiles(): gathered = jnp.take(padded, local_nbr, axis=0)]
    ppermute x16 -> x0, waiting for transfers between devices: 28.2 us -> none  [the longest x8 16.1 us: shifted(): return lax.ppermute(block, axis, route)]
  transfers between devices with their start and end apart: 24 -> 0, of which waited for: 22 -> 0; matrix products, arithmetic and copies ran while one was open for 0% -> 0% of each run, Pallas kernels for 0% -> 0%
where the time goes in v1:
time: 183 us
  Pallas kernels  174 us (95%)
  other arithmetic  4.91 us (3%)
  local copies, waits for them, and re-layouts  3.29 us (2%)
    pallas_call x1, Pallas kernels, shards(): pl.pallas_call(functools.partial(kernel, g), out_shape=jax.ShapeDtypeStru...  174 us

profile of v1, /device:TPU:1, one launch (start us, length us, event | category | flops | bytes accessed | tf_op | source)
XLA Modules:
  0.0 183.1 jit_solution(12276805207014865325)
XLA Ops:
  0.7 0.1 slice.11
  0.8 0.7 reduce
  1.5 0.7 reduce.1
  2.2 0.2 slice.10
  2.4 0.2 slice.9
  2.6 0.8 dynamic-slice_subtract_fusion
  3.4 0.1 copy.10
  3.5 0.1 sub.112
  3.6 0.1 convert_reduce_fusion.8
  3.7 0.1 select_reduce_fusion.10
  3.8 0.1 convert_reduce_fusion.7
  4.0 0.1 select_reduce_fusion.9
  4.1 0.2 convert_reduce_fusion.6
  4.2 0.1 select_reduce_fusion.6
  4.4 0.1 convert_reduce_fusion.2
  4.5 0.1 convert_reduce_fusion.4
  4.6 0.1 select_reduce_fusion.11
  4.7 0.1 convert_reduce_fusion.5
  4.9 0.1 select_reduce_fusion.8
  5.0 0.1 convert_reduce_fusion.3
  5.2 0.1 select_reduce_fusion.4
  5.3 0.1 select_reduce_fusion.5
  5.3 0.2 convert_reduce_fusion
  5.6 0.3 select_reduce_fusion
  5.9 0.2 convert_reduce_fusion.1
  6.1 0.3 select_reduce_fusion.2
  6.4 0.1 concatenate.3.idx
  6.5 0.0 copy-start
  6.5 1.0 copy-done
  7.5 0.0 copy-start.1
  7.5 0.7 copy-done.1
  8.2 174.1 %shard_map.82 = bf16[48,32,128]{2,1,0:T(8,128)(2,1)S(1)} custom-call(s32[2473]{0:T(1024)S(1)} %concatenate.3.idx, bf16[48,32,128]{2,1,0:T(8,128)(2,1)S(1)} %copy-done, bf16[48,8,128,128]{3,2,1,0:T(8,128)(2,1)} %prior.1, bf16[384,128,128]{2,1,0:T(8,128)(2,1)} %bitcast.3, f32[32,128]{1,0:T(8,128)S(1)} %copy-done.1), custom_call_target="tpu_custom_call" | custom-call | tf_op jit(solution)/shard_map/pallas_call | solution.py:294
  182.4 0.7 copy.13
  (22 shorter events, 0.2 us)
Async XLA Ops:
  6.5 1.0 copy-start
  7.5 0.7 copy-start.1

commit v2 on v1

v2 whole, which is shorter than its diff:
```python
import functools

import jax
import jax.numpy as jnp
from jax import lax
from jax.experimental import pallas as pl
from jax.experimental.pallas import tpu as pltpu
from jax.sharding import PartitionSpec as P

STEPS = 4
REACH = 12
FLUX_MINOR = 4
SIDE = 2
MESH = pl.DeviceIdType.MESH
F32 = jnp.float32
BF16 = jnp.bfloat16


def segment_pairs(key, lhs, segments, zero_lhs, pairs):
    count = key.shape[0]
    order = jnp.arange(count, dtype=jnp.int32)
    names = jnp.arange(segments, dtype=jnp.int32)
    hot = (key[:, None] == names[None, :]).astype(jnp.int32)
    size = jnp.sum(hot, axis=0)
    even = (size + 1) // 2 * 2
    begin = jnp.sum(jnp.where(names[None, :] < names[:, None], even[None, :], 0), axis=1)
    same = (key[None, :] == key[:, None]) & (order[None, :] < order[:, None])
    rank = jnp.sum(same.astype(jnp.int32), axis=1)
    place = jnp.where(key < segments, jnp.sum(hot * begin[None, :], axis=1) + rank, -1)
    slots = jnp.arange(2 * pairs, dtype=jnp.int32)
    match = slots[:, None] == place[None, :]
    block = jnp.sum(jnp.where(match, order[None, :], 0), axis=1)
    left = zero_lhs + jnp.sum(jnp.where(match, lhs[None, :] - zero_lhs, 0), axis=1)
    opens = (slots[::2][:, None] == begin[None, :]) & (size > 0)[None, :]
    flag = 1 - jnp.sum(opens.astype(jnp.int32), axis=1)
    last = jnp.where(size > 0, (begin + even) // 2 - 1, pairs)
    return jnp.concatenate([block, left, flag, last]).astype(jnp.int32)


def unroll_of(total, most):
    return max(u for u in range(1, most + 1) if total % u == 0)


def kernel(
    g, idx, probes, prior, jac, rinv, out,
    blocks, flipped, prior_own, prior_flip, ext_a, ext_b, spread_a, spread_b, weighted_a, weighted_b, adjoint_a, adjoint_b, scan,
    part_obs, got_obs, part_cell, got_cell, part_field, got_field,
    load_sem, fs, fr, ws, wr, os_, or_, gs, gr, cs, cr, es, er,
):
    no, nf, chunk = g["no"], g["nf"], g["chunk"]
    tiles, obs_blocks, nbrs, slots = g["tiles"], g["obs_blocks"], g["nbrs"], g["slots"]
    mine = obs_blocks // nf
    reach = (2 * SIDE + 1) * chunk
    ext, spread = (ext_a, ext_b), (spread_a, spread_b)
    weighted, adjoint = (weighted_a, weighted_b), (adjoint_a, adjoint_b)
    rows = ext_a.shape[1]
    o = lax.axis_index("obs")
    f = lax.axis_index("flux")
    chunks = no * nf

    def chunk_of(o_, f_):
        odd = lax.rem(f_, 2)
        return odd * (no - 1 - o_) + (1 - odd) * o_

    c = chunk_of(o, f)
    q = f * no + c

    def holder(distance):
        at = lax.rem(q + distance + chunks, chunks)
        f_ = lax.div(at, no)
        return (chunk_of(lax.rem(at, no), f_), f_)

    def flux_peer(r):
        y = g["flux_minor"]
        dz, dy = r
        z_ = lax.rem(lax.div(f, y) + dz, nf // y)
        y_ = lax.rem(lax.rem(f, y) + dy, y)
        return (o, z_ * y + y_)

    def obs_peer(r):
        return (lax.rem(o + r, no), f)

    def hops(d, n):
        return min(d, n - d)

    y = g["flux_minor"]
    far = [(dz, dy) for dz in range(nf // y) for dy in range(y) if dz + dy > 0]
    far.sort(key=lambda r: (-hops(r[0], nf // y) - hops(r[1], y), r))
    around = sorted(range(1, no), key=lambda r: (-hops(r, no), r))
    sides = [d for d in range(-SIDE, SIDE + 1) if d != 0]

    load_jac = pltpu.make_async_copy(jac, blocks, load_sem.at[0])
    load_prior = pltpu.make_async_copy(prior.at[pl.ds(c * chunk, chunk)], prior_own, load_sem.at[1])
    load_field = [
        pltpu.make_async_copy(
            probes.at[pl.ds(c * chunk, chunk), pl.ds(h * rows, rows)],
            ext[h].at[pl.ds(SIDE * chunk, chunk)], load_sem.at[2 + h],
        )
        for h in range(2)
    ]
    for copy in load_field:
        copy.start()
    load_prior.start()
    load_jac.start()

    barrier = pltpu.get_barrier_semaphore()
    partners = [flux_peer(r) for r in far] + [obs_peer(r) for r in around]
    partners += [holder(d) for d in sides]
    for partner in partners:
        pl.semaphore_signal(barrier, inc=1, device_id=partner, device_id_type=MESH)
    pl.semaphore_wait(barrier, len(partners))

    zero = jnp.zeros(spread_a.shape[1:], BF16)
    for h in range(2):
        spread[h][tiles] = zero
        weighted[h][obs_blocks] = zero
        adjoint[h][chunk] = zero

    def remote(src, dst, send, recv, device):
        return pltpu.make_async_remote_copy(
            src_ref=src, dst_ref=dst, send_sem=send, recv_sem=recv, device_id=device, device_id_type=MESH
        )

    def start_all(copies):
        for copy in copies:
            copy.start()

    def arrived(copies):
        for copy in copies:
            copy.wait_recv()

    def left(copies):
        for copy in copies:
            copy.wait_send()

    def products(h, base, pairs, lhs_ref, rhs_ref, unroll):
        def one(m, acc):
            a, b = base + 2 * m, base + 2 * m + 1
            lhs = jnp.concatenate([lhs_ref[h][idx[2 * pairs + a]], lhs_ref[h][idx[2 * pairs + b]]], axis=1)
            rhs = jnp.concatenate([rhs_ref[idx[a]], rhs_ref[idx[b]]], axis=0)
            acc = acc * idx[base + 4 * pairs + m].astype(F32)
            acc = acc + jnp.dot(lhs, rhs, preferred_element_type=F32)
            scan[h, m] = acc
            return acc

        def some(i, acc):
            for u in range(unroll):
                acc = one(i * unroll + u, acc)
            return acc

        lax.fori_loop(0, pairs // unroll, some, jnp.zeros(scan.shape[2:], F32))
        scan[h, pairs] = jnp.zeros(scan.shape[2:], F32)

    fwd_last = g["fwd_at"] + 5 * g["fwd_pairs"]
    adj_last = g["adj_at"] + 5 * g["adj_pairs"]
    gat_last = g["gat_at"] + 5 * g["gat_pairs"]

    def field_copies(h):
        own = ext[h].at[pl.ds(SIDE * chunk, chunk)]
        return [
            remote(own, ext[h].at[pl.ds((SIDE - d) * chunk, chunk)], es.at[h, i], er.at[h, i], holder(d))
            for i, d in enumerate(sides)
        ]

    def gather_copies(h):
        own = spread[h].at[pl.ds(c * chunk, chunk)]
        return [remote(own, own, gs.at[h, i], gr.at[h, i], obs_peer(r)) for i, r in enumerate(around)]

    def predicted_copies(h):
        copies = []
        for i, r in enumerate(far):
            peer = flux_peer(r)
            part = part_obs.at[h, pl.ds(peer[1] * mine, mine)]
            copies.append(remote(part, got_obs.at[h, i], fs.at[h, i], fr.at[h, i], peer))
        return copies

    def weighted_copies(h):
        own = weighted[h].at[pl.ds(f * mine, mine)]
        return [remote(own, own, ws.at[h, i], wr.at[h, i], flux_peer(r)) for i, r in enumerate(far)]

    def cell_copies(h):
        copies = []
        for i, r in enumerate(around):
            peer = obs_peer(r)
            part = part_cell.at[h, pl.ds(chunk_of(peer[0], f) * chunk, chunk)]
            copies.append(remote(part, got_cell.at[h, i], os_.at[h, i], or_.at[h, i], peer))
        return copies

    def contribution_copies(h):
        return [
            remote(
                part_field.at[h, pl.ds((SIDE + d) * chunk, chunk)], got_field.at[h, i],
                cs.at[h, i], cr.at[h, i], holder(d),
            )
            for i, d in enumerate(sides)
        ]

    def spread_phase(h, s):
        copies = field_copies(h)
        if h == 0:
            @pl.when(s == 0)
            def _():
                load_prior.wait()

        arrived(copies)
        for t in range(chunk):
            lhs = jnp.concatenate([ext[h][idx[g["nbr_at"] + t * nbrs + k]] for k in range(nbrs)], axis=1)
            rhs = prior_own[t].reshape(nbrs * prior_own.shape[2], prior_own.shape[3])
            spread[h][c * chunk + t] = jnp.dot(lhs, rhs, preferred_element_type=F32).astype(BF16)
        start_all(gather_copies(h))
        left(copies)

    def forward_phase(h, s):
        copies = gather_copies(h)
        if h == 0:
            @pl.when(s == 0)
            def _():
                for e in range(chunk * nbrs):
                    prior_flip[e] = prior_own[e // nbrs, e % nbrs].T
                load_jac.wait()

        arrived(copies)
        products(h, g["fwd_at"], g["fwd_pairs"], spread, blocks, g["fwd_unroll"])
        for b in range(obs_blocks):
            part_obs[h, b] = scan[h, idx[fwd_last + b]].astype(BF16)
        start_all(predicted_copies(h))
        left(copies)

    def weight_phase(h, s):
        copies = predicted_copies(h)
        if h == 0:
            @pl.when(s == 0)
            def _():
                many = unroll_of(slots, 8)

                def flip(i, carry):
                    for u in range(many):
                        flipped[i * many + u] = blocks[i * many + u].T
                    return carry

                lax.fori_loop(0, slots // many, flip, 0)

        arrived(copies)
        for b in range(mine):
            total = scan[h, idx[fwd_last + f * mine + b]]
            for i in range(len(far)):
                total = total + got_obs[h, i, b].astype(F32)
            weighted[h][f * mine + b] = (total * rinv[pl.ds(f * mine + b, 1), :]).astype(BF16)
        start_all(weighted_copies(h))
        left(copies)

    def adjoint_phase(h, s):
        copies = weighted_copies(h)
        arrived(copies)
        products(h, g["adj_at"], g["adj_pairs"], weighted, flipped, g["adj_unroll"])
        for t in range(tiles):
            part_cell[h, t] = scan[h, idx[adj_last + t]].astype(BF16)
        start_all(cell_copies(h))
        left(copies)

    def prior_phase(h, s):
        copies = cell_copies(h)
        arrived(copies)
        for t in range(chunk):
            total = scan[h, idx[adj_last + c * chunk + t]]
            for i in range(len(around)):
                total = total + got_cell[h, i, t].astype(F32)
            adjoint[h][t] = total.astype(BF16)
        products(h, g["gat_at"], g["gat_pairs"], adjoint, prior_flip, g["gat_unroll"])
        for j in range(reach):
            if j // chunk != SIDE:
                part_field[h, j] = scan[h, idx[gat_last + j]].astype(BF16)
        start_all(contribution_copies(h))
        left(copies)

    def field_phase(h, s):
        copies = contribution_copies(h)
        arrived(copies)
        for t in range(chunk):
            total = scan[h, idx[gat_last + SIDE * chunk + t]]
            for i in range(len(sides)):
                total = total + got_field[h, i, t].astype(F32)
            ext[h][SIDE * chunk + t] = total.astype(BF16)

        @pl.when(s < STEPS - 1)
        def _():
            start_all(field_copies(h))

        left(copies)

    for h in range(2):
        load_field[h].wait()
        start_all(field_copies(h))

    def step(s, carry):
        for phase in (spread_phase, forward_phase, weight_phase, adjoint_phase, prior_phase, field_phase):
            for h in range(2):
                phase(h, s)
        return carry

    lax.fori_loop(0, STEPS, step, 0)
    for h in range(2):
        for t in range(chunk):
            spread[h][c * chunk + t] = ext[h][SIDE * chunk + t]
        start_all(gather_copies(h))
    for h in range(2):
        copies = gather_copies(h)
        arrived(copies)
        left(copies)
        out[:, pl.ds(h * rows, rows), :] = spread[h][pl.ds(0, tiles)]


def shards(no, nf, flux_minor, probes, prior_tiles, neighbours, jac, jac_obs, jac_flux, counts, rinv):
    tiles, probe_count, width = probes.shape
    nbrs = prior_tiles.shape[1]
    obs_blocks = rinv.shape[0]
    slots = jac.shape[2]
    chunk = tiles // no
    assert SIDE * chunk == REACH and obs_blocks % nf == 0
    reach = (2 * SIDE + 1) * chunk
    fwd_pairs = (slots + obs_blocks) // 2
    adj_pairs = (slots + tiles) // 2
    gat_pairs = (chunk * nbrs + reach) // 2
    o = lax.axis_index("obs")
    f = lax.axis_index("flux")
    c = jnp.where(f % 2 == 1, no - 1 - o, o)
    live = jnp.arange(slots, dtype=jnp.int32) < counts[0, 0]
    block_obs, block_flux = jac_obs[0, 0], jac_flux[0, 0]
    own = lax.dynamic_slice_in_dim(neighbours, c * chunk, chunk, 0).reshape(-1)
    own = own - (f * tiles + c * chunk - SIDE * chunk)
    entry_tile = jnp.arange(chunk * nbrs, dtype=jnp.int32) // nbrs
    fwd = segment_pairs(jnp.where(live, block_obs, obs_blocks), block_flux, obs_blocks, tiles, fwd_pairs)
    adj = segment_pairs(jnp.where(live, block_flux, tiles), block_obs, tiles, obs_blocks, adj_pairs)
    gat = segment_pairs(own, entry_tile, reach, chunk, gat_pairs)
    idx = jnp.concatenate([fwd, adj, gat, own])
    g = dict(
        no=no, nf=nf, flux_minor=flux_minor, chunk=chunk, tiles=tiles, obs_blocks=obs_blocks, nbrs=nbrs, slots=slots,
        fwd_pairs=fwd_pairs, adj_pairs=adj_pairs, gat_pairs=gat_pairs,
        fwd_at=0, adj_at=fwd.shape[0], gat_at=fwd.shape[0] + adj.shape[0],
        nbr_at=fwd.shape[0] + adj.shape[0] + gat.shape[0],
        fwd_unroll=unroll_of(fwd_pairs, 108), adj_unroll=unroll_of(adj_pairs, 108),
        gat_unroll=unroll_of(gat_pairs, 56),
    )
    mine = obs_blocks // nf
    tile = (probe_count, width)
    half = (probe_count // 2, width)
    dma = pltpu.SemaphoreType.DMA
    most = max(fwd_pairs, adj_pairs, gat_pairs) + 1
    vmem = pl.BlockSpec(memory_space=pltpu.VMEM)
    any_space = pl.BlockSpec(memory_space=pl.ANY)
    return pl.pallas_call(
        functools.partial(kernel, g),
        out_shape=jax.ShapeDtypeStruct((tiles,) + tile, BF16),
        in_specs=[pl.BlockSpec(memory_space=pltpu.SMEM), any_space, any_space, any_space, vmem],
        out_specs=vmem,
        scratch_shapes=[
            pltpu.VMEM((slots, width, width), BF16),
            pltpu.VMEM((slots, width, width), BF16),
            pltpu.VMEM((chunk, nbrs, width, width), BF16),
            pltpu.VMEM((chunk * nbrs, width, width), BF16),
            pltpu.VMEM((reach,) + half, BF16), pltpu.VMEM((reach,) + half, BF16),
            pltpu.VMEM((tiles + 1,) + half, BF16), pltpu.VMEM((tiles + 1,) + half, BF16),
            pltpu.VMEM((obs_blocks + 1,) + half, BF16), pltpu.VMEM((obs_blocks + 1,) + half, BF16),
            pltpu.VMEM((chunk + 1,) + half, BF16), pltpu.VMEM((chunk + 1,) + half, BF16),
            pltpu.VMEM((2, most) + half, F32),
            pltpu.VMEM((2, obs_blocks) + half, BF16),
            pltpu.VMEM((2, nf - 1, mine) + half, BF16),
            pltpu.VMEM((2, tiles) + half, BF16),
            pltpu.VMEM((2, no - 1, chunk) + half, BF16),
            pltpu.VMEM((2, reach) + half, BF16),
            pltpu.VMEM((2, 2 * SIDE, chunk) + half, BF16),
            dma((4,)),
            dma((2, nf - 1)), dma((2, nf - 1)), dma((2, nf - 1)), dma((2, nf - 1)),
            dma((2, no - 1)), dma((2, no - 1)), dma((2, no - 1)), dma((2, no - 1)),
            dma((2, 2 * SIDE)), dma((2, 2 * SIDE)), dma((2, 2 * SIDE)), dma((2, 2 * SIDE)),
        ],
        compiler_params=pltpu.CompilerParams(
            collective_id=0, has_side_effects=True, vmem_limit_bytes=48 * 1024 * 1024
        ),
    )(idx, probes, prior_tiles, jac[0, 0], rinv)


def solution(mesh):
    placed = (
        P("flux", None, None),
        P("flux", None, None, None),
        P("flux", None),
        P("obs", "flux", None, None, None),
        P("obs", "flux", None),
        P("obs", "flux", None),
        P("obs", "flux"),
        P("obs", None),
    )
    return jax.shard_map(
        functools.partial(shards, mesh.shape["obs"], mesh.shape["flux"], FLUX_MINOR),
        mesh=mesh, in_specs=placed, out_specs=P("flux", None, None), check_vma=False,
    )
```

time: 183 us -> 161 us (0.88)
  Pallas kernels: 174 us -> 151 us
    pallas_call x1, Pallas kernels: 174 us -> 151 us  [shards(): pl.pallas_call(functools.partial(kernel, g), out_shape=jax.ShapeDtypeStru...]
where the time goes in v2:
time: 161 us; the launch traced here: 160 us
  Pallas kernels  151 us (94%)
  other arithmetic  4.91 us (3%)
  local copies, waits for them, and re-layouts  3.29 us (2%)
    pallas_call x1, Pallas kernels, shards(): pl.pallas_call(functools.partial(kernel, g), out_shape=jax.ShapeDtypeStru...  151 us

profile of v2, /device:TPU:1, one launch (start us, length us, event | category | flops | bytes accessed | tf_op | source)
XLA Modules:
  0.0 160.3 jit_solution(436495424148173451)
XLA Ops:
  0.7 0.1 slice.11
  0.8 0.7 reduce
  1.5 0.7 reduce.1
  2.2 0.2 slice.10
  2.4 0.2 slice.9
  2.6 0.8 dynamic-slice_subtract_fusion
  3.4 0.1 copy.10
  3.5 0.1 sub.112
  3.6 0.1 convert_reduce_fusion.8
  3.7 0.1 select_reduce_fusion.10
  3.8 0.1 convert_reduce_fusion.7
  4.0 0.1 select_reduce_fusion.9
  4.1 0.2 convert_reduce_fusion.6
  4.2 0.1 select_reduce_fusion.6
  4.4 0.1 convert_reduce_fusion.2
  4.5 0.1 convert_reduce_fusion.4
  4.6 0.1 select_reduce_fusion.11
  4.7 0.1 convert_reduce_fusion.5
  4.9 0.1 select_reduce_fusion.8
  5.0 0.1 convert_reduce_fusion.3
  5.2 0.1 select_reduce_fusion.4
  5.3 0.1 select_reduce_fusion.5
  5.3 0.2 convert_reduce_fusion
  5.6 0.3 select_reduce_fusion
  5.9 0.2 convert_reduce_fusion.1
  6.1 0.3 select_reduce_fusion.2
  6.4 0.1 concatenate.3.idx
  6.5 0.0 copy-start
  6.5 1.0 copy-done
  7.5 0.0 copy-start.1
  7.5 0.7 copy-done.1
  8.2 151.3 %shard_map.82 = bf16[48,32,128]{2,1,0:T(8,128)(2,1)S(1)} custom-call(s32[2473]{0:T(1024)S(1)} %concatenate.3.idx, bf16[48,32,128]{2,1,0:T(8,128)(2,1)S(1)} %copy-done, bf16[48,8,128,128]{3,2,1,0:T(8,128)(2,1)} %prior.1, bf16[384,128,128]{2,1,0:T(8,128)(2,1)} %bitcast.3, f32[32,128]{1,0:T(8,128)S(1)} %copy-done.1), custom_call_target="tpu_custom_call" | custom-call | tf_op jit(solution)/shard_map/pallas_call | solution.py:351
  159.5 0.7 copy.13
  (22 shorter events, 0.2 us)
Async XLA Ops:
  6.5 1.0 copy-start
  7.5 0.7 copy-start.1

commit v3 on v2

--- a/solution.py
+++ b/solution.py
@@ -125,13 +125,23 @@
         for copy in copies:
             copy.start()
 
-    def arrived(copies):
-        for copy in copies:
-            copy.wait_recv()
-
-    def left(copies):
-        for copy in copies:
-            copy.wait_send()
+    def field_all(h):
+        return remote(*[ext[h].at[pl.ds(0, len(sides) * chunk)]] * 2, es.at[h], er.at[h], holder(1))
+
+    def gather_all(h):
+        return remote(*[spread[h].at[pl.ds(0, len(around) * chunk)]] * 2, gs.at[h], gr.at[h], obs_peer(1))
+
+    def predicted_all(h):
+        return remote(got_obs.at[h], got_obs.at[h], fs.at[h], fr.at[h], obs_peer(1))
+
+    def weighted_all(h):
+        return remote(*[weighted[h].at[pl.ds(0, len(far) * mine)]] * 2, ws.at[h], wr.at[h], obs_peer(1))
+
+    def cell_all(h):
+        return remote(got_cell.at[h], got_cell.at[h], os_.at[h], or_.at[h], obs_peer(1))
+
+    def contribution_all(h):
+        return remote(got_field.at[h], got_field.at[h], cs.at[h], cr.at[h], obs_peer(1))
 
     def products(h, base, pairs, lhs_ref, rhs_ref, unroll):
         def one(m, acc):
@@ -158,60 +168,60 @@
     def field_copies(h):
         own = ext[h].at[pl.ds(SIDE * chunk, chunk)]
         return [
-            remote(own, ext[h].at[pl.ds((SIDE - d) * chunk, chunk)], es.at[h, i], er.at[h, i], holder(d))
+            remote(own, ext[h].at[pl.ds((SIDE - d) * chunk, chunk)], es.at[h], er.at[h], holder(d))
             for i, d in enumerate(sides)
         ]
 
     def gather_copies(h):
         own = spread[h].at[pl.ds(c * chunk, chunk)]
-        return [remote(own, own, gs.at[h, i], gr.at[h, i], obs_peer(r)) for i, r in enumerate(around)]
+        return [remote(own, own, gs.at[h], gr.at[h], obs_peer(r)) for i, r in enumerate(around)]
 
     def predicted_copies(h):
         copies = []
         for i, r in enumerate(far):
             peer = flux_peer(r)
             part = part_obs.at[h, pl.ds(peer[1] * mine, mine)]
-            copies.append(remote(part, got_obs.at[h, i], fs.at[h, i], fr.at[h, i], peer))
+            copies.append(remote(part, got_obs.at[h, i], fs.at[h], fr.at[h], peer))
         return copies
 
     def weighted_copies(h):
         own = weighted[h].at[pl.ds(f * mine, mine)]
-        return [remote(own, own, ws.at[h, i], wr.at[h, i], flux_peer(r)) for i, r in enumerate(far)]
+        return [remote(own, own, ws.at[h], wr.at[h], flux_peer(r)) for i, r in enumerate(far)]
 
     def cell_copies(h):
         copies = []
         for i, r in enumerate(around):
             peer = obs_peer(r)
             part = part_cell.at[h, pl.ds(chunk_of(peer[0], f) * chunk, chunk)]
-            copies.append(remote(part, got_cell.at[h, i], os_.at[h, i], or_.at[h, i], peer))
+            copies.append(remote(part, got_cell.at[h, i], os_.at[h], or_.at[h], peer))
         return copies
 
     def contribution_copies(h):
         return [
             remote(
                 part_field.at[h, pl.ds((SIDE + d) * chunk, chunk)], got_field.at[h, i],
-                cs.at[h, i], cr.at[h, i], holder(d),
+                cs.at[h], cr.at[h], holder(d),
             )
             for i, d in enumerate(sides)
         ]
 
     def spread_phase(h, s):
-        copies = field_copies(h)
+        every = field_all(h)
         if h == 0:
             @pl.when(s == 0)
             def _():
                 load_prior.wait()
 
-        arrived(copies)
+        every.wait_recv()
         for t in range(chunk):
             lhs = jnp.concatenate([ext[h][idx[g["nbr_at"] + t * nbrs + k]] for k in range(nbrs)], axis=1)
             rhs = prior_own[t].reshape(nbrs * prior_own.shape[2], prior_own.shape[3])
             spread[h][c * chunk + t] = jnp.dot(lhs, rhs, preferred_element_type=F32).astype(BF16)
         start_all(gather_copies(h))
-        left(copies)
+        every.wait_send()
 
     def forward_phase(h, s):
-        copies = gather_copies(h)
+        every = gather_all(h)
         if h == 0:
             @pl.when(s == 0)
             def _():
@@ -219,15 +229,15 @@
                     prior_flip[e] = prior_own[e // nbrs, e % nbrs].T
                 load_jac.wait()
 
-        arrived(copies)
+        every.wait_recv()
         products(h, g["fwd_at"], g["fwd_pairs"], spread, blocks, g["fwd_unroll"])
         for b in range(obs_blocks):
             part_obs[h, b] = scan[h, idx[fwd_last + b]].astype(BF16)
         start_all(predicted_copies(h))
-        left(copies)
+        every.wait_send()
 
     def weight_phase(h, s):
-        copies = predicted_copies(h)
+        every = predicted_all(h)
         if h == 0:
             @pl.when(s == 0)
             def _():
@@ -240,27 +250,27 @@
 
                 lax.fori_loop(0, slots // many, flip, 0)
 
-        arrived(copies)
+        every.wait_recv()
         for b in range(mine):
             total = scan[h, idx[fwd_last + f * mine + b]]
             for i in range(len(far)):
                 total = total + got_obs[h, i, b].astype(F32)
             weighted[h][f * mine + b] = (total * rinv[pl.ds(f * mine + b, 1), :]).astype(BF16)
         start_all(weighted_copies(h))
-        left(copies)
+        every.wait_send()
 
     def adjoint_phase(h, s):
-        copies = weighted_copies(h)
-        arrived(copies)
+        every = weighted_all(h)
+        every.wait_recv()
         products(h, g["adj_at"], g["adj_pairs"], weighted, flipped, g["adj_unroll"])
         for t in range(tiles):
             part_cell[h, t] = scan[h, idx[adj_last + t]].astype(BF16)
         start_all(cell_copies(h))
-        left(copies)
+        every.wait_send()
 
     def prior_phase(h, s):
-        copies = cell_copies(h)
-        arrived(copies)
+        every = cell_all(h)
+        every.wait_recv()
         for t in range(chunk):
             total = scan[h, idx[adj_last + c * chunk + t]]
             for i in range(len(around)):
@@ -271,11 +281,11 @@
             if j // chunk != SIDE:
                 part_field[h, j] = scan[h, idx[gat_last + j]].astype(BF16)
         start_all(contribution_copies(h))
-        left(copies)
+        every.wait_send()
 
     def field_phase(h, s):
-        copies = contribution_copies(h)
-        arrived(copies)
+        every = contribution_all(h)
+        every.wait_recv()
         for t in range(chunk):
             total = scan[h, idx[gat_last + SIDE * chunk + t]]
             for i in range(len(sides)):
@@ -286,7 +296,7 @@
         def _():
             start_all(field_copies(h))
 
-        left(copies)
+        every.wait_send()
 
     for h in range(2):
         load_field[h].wait()
@@ -304,9 +314,9 @@
             spread[h][c * chunk + t] = ext[h][SIDE * chunk + t]
         start_all(gather_copies(h))
     for h in range(2):
-        copies = gather_copies(h)
-        arrived(copies)
-        left(copies)
+        every = gather_all(h)
+        every.wait_recv()
+        every.wait_send()
         out[:, pl.ds(h * rows, rows), :] = spread[h][pl.ds(0, tiles)]
 
 
@@ -370,9 +380,9 @@
             pltpu.VMEM((2, reach) + half, BF16),
             pltpu.VMEM((2, 2 * SIDE, chunk) + half, BF16),
             dma((4,)),
-            dma((2, nf - 1)), dma((2, nf - 1)), dma((2, nf - 1)), dma((2, nf - 1)),
-            dma((2, no - 1)), dma((2, no - 1)), dma((2, no - 1)), dma((2, no - 1)),
-            dma((2, 2 * SIDE)), dma((2, 2 * SIDE)), dma((2, 2 * SIDE)), dma((2, 2 * SIDE)),
+            dma((2,)), dma((2,)), dma((2,)), dma((2,)),
+            dma((2,)), dma((2,)), dma((2,)), dma((2,)),
+            dma((2,)), dma((2,)), dma((2,)), dma((2,)),
         ],
         compiler_params=pltpu.CompilerParams(
             collective_id=0, has_side_effects=True, vmem_limit_bytes=48 * 1024 * 1024

time: 161 us -> 159 us (0.988)
  Pallas kernels: 151 us -> 149 us
    pallas_call x1, Pallas kernels: 151 us -> 149 us  [shards(): pl.pallas_call(functools.partial(kernel, g), out_shape=jax.ShapeDtypeStru...]
where the time goes in v3:
time: 159 us; the launch traced here: 158 us
  Pallas kernels  149 us (94%)
  other arithmetic  4.91 us (3%)
  local copies, waits for them, and re-layouts  3.29 us (2%)
    pallas_call x1, Pallas kernels, shards(): pl.pallas_call(functools.partial(kernel, g), out_shape=jax.ShapeDtypeStru...  149 us

profile of v3, /device:TPU:1, one launch (start us, length us, event | category | flops | bytes accessed | tf_op | source)
XLA Modules:
  0.0 158.4 jit_solution(11801743279555661382)
XLA Ops:
  0.7 0.1 slice.11
  0.8 0.7 reduce
  1.5 0.7 reduce.1
  2.2 0.2 slice.10
  2.4 0.2 slice.9
  2.6 0.8 dynamic-slice_subtract_fusion
  3.4 0.1 copy.10
  3.5 0.1 sub.112
  3.6 0.1 convert_reduce_fusion.8
  3.7 0.1 select_reduce_fusion.10
  3.8 0.1 convert_reduce_fusion.7
  4.0 0.1 select_reduce_fusion.9
  4.1 0.2 convert_reduce_fusion.6
  4.2 0.1 select_reduce_fusion.6
  4.4 0.1 convert_reduce_fusion.2
  4.5 0.1 convert_reduce_fusion.4
  4.6 0.1 select_reduce_fusion.11
  4.7 0.1 convert_reduce_fusion.5
  4.9 0.1 select_reduce_fusion.8
  5.0 0.1 convert_reduce_fusion.3
  5.2 0.1 select_reduce_fusion.4
  5.3 0.1 select_reduce_fusion.5
  5.3 0.2 convert_reduce_fusion
  5.6 0.3 select_reduce_fusion
  5.9 0.2 convert_reduce_fusion.1
  6.1 0.3 select_reduce_fusion.2
  6.4 0.1 concatenate.3.idx
  6.5 0.0 copy-start
  6.5 1.0 copy-done
  7.5 0.0 copy-start.1
  7.5 0.7 copy-done.1
  8.2 149.4 %shard_map.82 = bf16[48,32,128]{2,1,0:T(8,128)(2,1)S(1)} custom-call(s32[2473]{0:T(1024)S(1)} %concatenate.3.idx, bf16[48,32,128]{2,1,0:T(8,128)(2,1)S(1)} %copy-done, bf16[48,8,128,128]{3,2,1,0:T(8,128)(2,1)} %prior.1, bf16[384,128,128]{2,1,0:T(8,128)(2,1)} %bitcast.3, f32[32,128]{1,0:T(8,128)S(1)} %copy-done.1), custom_call_target="tpu_custom_call" | custom-call | tf_op jit(solution)/shard_map/pallas_call | solution.py:361
  157.7 0.7 copy.13
  (22 shorter events, 0.2 us)
Async XLA Ops:
  6.5 1.0 copy-start
  7.5 0.7 copy-start.1

commit v4 on v3

--- a/solution.py
+++ b/solution.py
@@ -16,25 +16,49 @@
 BF16 = jnp.bfloat16
 
 
-def segment_pairs(key, lhs, segments, zero_lhs, pairs):
-    count = key.shape[0]
-    order = jnp.arange(count, dtype=jnp.int32)
-    names = jnp.arange(segments, dtype=jnp.int32)
-    hot = (key[:, None] == names[None, :]).astype(jnp.int32)
-    size = jnp.sum(hot, axis=0)
-    even = (size + 1) // 2 * 2
-    begin = jnp.sum(jnp.where(names[None, :] < names[:, None], even[None, :], 0), axis=1)
-    same = (key[None, :] == key[:, None]) & (order[None, :] < order[:, None])
-    rank = jnp.sum(same.astype(jnp.int32), axis=1)
-    place = jnp.where(key < segments, jnp.sum(hot * begin[None, :], axis=1) + rank, -1)
-    slots = jnp.arange(2 * pairs, dtype=jnp.int32)
-    match = slots[:, None] == place[None, :]
-    block = jnp.sum(jnp.where(match, order[None, :], 0), axis=1)
-    left = zero_lhs + jnp.sum(jnp.where(match, lhs[None, :] - zero_lhs, 0), axis=1)
-    opens = (slots[::2][:, None] == begin[None, :]) & (size > 0)[None, :]
-    flag = 1 - jnp.sum(opens.astype(jnp.int32), axis=1)
-    last = jnp.where(size > 0, (begin + even) // 2 - 1, pairs)
-    return jnp.concatenate([block, left, flag, last]).astype(jnp.int32)
+LANES = 128
+NOBODY = LANES - 1
+
+
+def iota(shape, dim):
+    return lax.broadcasted_iota(jnp.int32, shape, dim)
+
+
+def column(row):
+    parts = [
+        jnp.broadcast_to(row[:, i : i + LANES], (LANES, LANES)).T for i in range(0, row.shape[1], LANES)
+    ]
+    return jnp.concatenate(parts, axis=0) if len(parts) > 1 else parts[0]
+
+
+def total(values):
+    return jnp.sum(values, axis=0, keepdims=True)
+
+
+def segment_pairs(table, at, key, lhs, zero_lhs, pairs):
+    count = key.shape[1]
+    square = (LANES, LANES)
+    key_col = column(key)
+    size = total((key_col == iota((count, LANES), 1)).astype(jnp.int32))
+    even = ((size + 1) >> 1) << 1
+    begin = total(jnp.where(iota(square, 0) < iota(square, 1), column(even), 0))
+    begin_col, size_col = column(begin), column(size)
+    place = []
+    for i in range(0, count, LANES):
+        here = key[:, i : i + LANES]
+        first = total(jnp.where(iota(square, 0) == here, begin_col, 0))
+        same = (key_col == here) & (iota((count, LANES), 0) < iota((count, LANES), 1) + i)
+        place.append(first + total(same.astype(jnp.int32)))
+    place_col = column(jnp.concatenate(place, axis=1) if len(place) > 1 else place[0])
+    packed = jnp.where(key_col == NOBODY, 0, (column(lhs) + 1) * 1024 + iota((count, LANES), 0))
+    for i in range(0, 2 * pairs, LANES):
+        found = total(jnp.where(place_col == iota((count, LANES), 1) + i, packed, 0))
+        table[at : at + 1, i : i + LANES] = found & 1023
+        table[at + 1 : at + 2, i : i + LANES] = jnp.where(found == 0, zero_lhs, (found >> 10) - 1)
+    for i in range(0, 2 * LANES, LANES):
+        opens = (begin_col == 2 * (iota(square, 1) + i)) & (size_col > 0)
+        table[at + 2 : at + 3, i : i + LANES] = 1 - total(opens.astype(jnp.int32))
+    table[at + 2 : at + 3, 2 * LANES : 3 * LANES] = jnp.where(size > 0, ((begin + even) >> 1) - 1, pairs)
 
 
 def unroll_of(total, most):
@@ -42,7 +66,8 @@
 
 
 def kernel(
-    g, idx, probes, prior, jac, rinv, out,
+    g, near_in, obs_in, cell_in, counts_in, probes, prior, jac, rinv_in, out,
+    idx, table, near, obs_row, cell_row, count, rinv,
     blocks, flipped, prior_own, prior_flip, ext_a, ext_b, spread_a, spread_b, weighted_a, weighted_b, adjoint_a, adjoint_b, scan,
     part_obs, got_obs, part_cell, got_cell, part_field, got_field,
     load_sem, fs, fr, ws, wr, os_, or_, gs, gr, cs, cr, es, er,
@@ -98,7 +123,9 @@
         )
         for h in range(2)
     ]
-    for copy in load_field:
+    small = [(near_in, near), (obs_in, obs_row), (cell_in, cell_row), (counts_in, count), (rinv_in, rinv)]
+    load_small = [pltpu.make_async_copy(a, b, load_sem.at[5 + i]) for i, (a, b) in enumerate(small)]
+    for copy in load_small + load_field:
         copy.start()
     load_prior.start()
     load_jac.start()
@@ -108,6 +135,19 @@
     partners += [holder(d) for d in sides]
     for partner in partners:
         pl.semaphore_signal(barrier, inc=1, device_id=partner, device_id_type=MESH)
+
+    for copy in load_small:
+        copy.wait()
+    live = iota((1, slots), 1) < jnp.broadcast_to(count[...], (1, slots))
+    by_obs, by_cell = obs_row[0], cell_row[0]
+    segment_pairs(table, 0, jnp.where(live, by_obs, NOBODY), by_cell, tiles, g["fwd_pairs"])
+    segment_pairs(table, 3, jnp.where(live, by_cell, NOBODY), by_obs, obs_blocks, g["adj_pairs"])
+    entry = iota((1, LANES), 1)
+    by_near = jnp.where(entry < chunk * nbrs, near[...], NOBODY)
+    segment_pairs(table, 6, by_near, jnp.minimum(entry // nbrs, chunk - 1), chunk, g["gat_pairs"])
+    table[9:10, :LANES] = near[...]
+    load_index = pltpu.make_async_copy(table, idx, load_sem.at[4])
+    load_index.start()
     pl.semaphore_wait(barrier, len(partners))
 
     zero = jnp.zeros(spread_a.shape[1:], BF16)
@@ -145,10 +185,10 @@
 
     def products(h, base, pairs, lhs_ref, rhs_ref, unroll):
         def one(m, acc):
-            a, b = base + 2 * m, base + 2 * m + 1
-            lhs = jnp.concatenate([lhs_ref[h][idx[2 * pairs + a]], lhs_ref[h][idx[2 * pairs + b]]], axis=1)
-            rhs = jnp.concatenate([rhs_ref[idx[a]], rhs_ref[idx[b]]], axis=0)
-            acc = acc * idx[base + 4 * pairs + m].astype(F32)
+            a, b = 2 * m, 2 * m + 1
+            lhs = jnp.concatenate([lhs_ref[h][idx[base + 1, a]], lhs_ref[h][idx[base + 1, b]]], axis=1)
+            rhs = jnp.concatenate([rhs_ref[idx[base, a]], rhs_ref[idx[base, b]]], axis=0)
+            acc = acc * idx[base + 2, m].astype(F32)
             acc = acc + jnp.dot(lhs, rhs, preferred_element_type=F32)
             scan[h, m] = acc
             return acc
@@ -161,9 +201,8 @@
         lax.fori_loop(0, pairs // unroll, some, jnp.zeros(scan.shape[2:], F32))
         scan[h, pairs] = jnp.zeros(scan.shape[2:], F32)
 
-    fwd_last = g["fwd_at"] + 5 * g["fwd_pairs"]
-    adj_last = g["adj_at"] + 5 * g["adj_pairs"]
-    gat_last = g["gat_at"] + 5 * g["gat_pairs"]
+    def last_of(base, segment):
+        return idx[base + 2, 2 * LANES + segment]
 
     def field_copies(h):
         own = ext[h].at[pl.ds(SIDE * chunk, chunk)]
@@ -210,11 +249,12 @@
         if h == 0:
             @pl.when(s == 0)
             def _():
+                load_index.wait()
                 load_prior.wait()
 
         every.wait_recv()
         for t in range(chunk):
-            lhs = jnp.concatenate([ext[h][idx[g["nbr_at"] + t * nbrs + k]] for k in range(nbrs)], axis=1)
+            lhs = jnp.concatenate([ext[h][idx[9, t * nbrs + k]] for k in range(nbrs)], axis=1)
             rhs = prior_own[t].reshape(nbrs * prior_own.shape[2], prior_own.shape[3])
             spread[h][c * chunk + t] = jnp.dot(lhs, rhs, preferred_element_type=F32).astype(BF16)
         start_all(gather_copies(h))
@@ -230,9 +270,9 @@
                 load_jac.wait()
 
         every.wait_recv()
-        products(h, g["fwd_at"], g["fwd_pairs"], spread, blocks, g["fwd_unroll"])
+        products(h, 0, g["fwd_pairs"], spread, blocks, g["fwd_unroll"])
         for b in range(obs_blocks):
-            part_obs[h, b] = scan[h, idx[fwd_last + b]].astype(BF16)
+            part_obs[h, b] = scan[h, last_of(0, b)].astype(BF16)
         start_all(predicted_copies(h))
         every.wait_send()
 
@@ -252,19 +292,19 @@
 
         every.wait_recv()
         for b in range(mine):
-            total = scan[h, idx[fwd_last + f * mine + b]]
+            value = scan[h, last_of(0, f * mine + b)]
             for i in range(len(far)):
-                total = total + got_obs[h, i, b].astype(F32)
-            weighted[h][f * mine + b] = (total * rinv[pl.ds(f * mine + b, 1), :]).astype(BF16)
+                value = value + got_obs[h, i, b].astype(F32)
+            weighted[h][f * mine + b] = (value * rinv[pl.ds(f * mine + b, 1), :]).astype(BF16)
         start_all(weighted_copies(h))
         every.wait_send()
 
     def adjoint_phase(h, s):
         every = weighted_all(h)
         every.wait_recv()
-        products(h, g["adj_at"], g["adj_pairs"], weighted, flipped, g["adj_unroll"])
+        products(h, 3, g["adj_pairs"], weighted, flipped, g["adj_unroll"])
         for t in range(tiles):
-            part_cell[h, t] = scan[h, idx[adj_last + t]].astype(BF16)
+            part_cell[h, t] = scan[h, last_of(3, t)].astype(BF16)
         start_all(cell_copies(h))
         every.wait_send()
 
@@ -272,14 +312,14 @@
         every = cell_all(h)
         every.wait_recv()
         for t in range(chunk):
-            total = scan[h, idx[adj_last + c * chunk + t]]
+            value = scan[h, last_of(3, c * chunk + t)]
             for i in range(len(around)):
-                total = total + got_cell[h, i, t].astype(F32)
-            adjoint[h][t] = total.astype(BF16)
-        products(h, g["gat_at"], g["gat_pairs"], adjoint, prior_flip, g["gat_unroll"])
+                value = value + got_cell[h, i, t].astype(F32)
+            adjoint[h][t] = value.astype(BF16)
+        products(h, 6, g["gat_pairs"], adjoint, prior_flip, g["gat_unroll"])
         for j in range(reach):
             if j // chunk != SIDE:
-                part_field[h, j] = scan[h, idx[gat_last + j]].astype(BF16)
+                part_field[h, j] = scan[h, last_of(6, j)].astype(BF16)
         start_all(contribution_copies(h))
         every.wait_send()
 
@@ -287,10 +327,10 @@
         every = contribution_all(h)
         every.wait_recv()
         for t in range(chunk):
-            total = scan[h, idx[gat_last + SIDE * chunk + t]]
+            value = scan[h, last_of(6, SIDE * chunk + t)]
             for i in range(len(sides)):
-                total = total + got_field[h, i, t].astype(F32)
-            ext[h][SIDE * chunk + t] = total.astype(BF16)
+                value = value + got_field[h, i, t].astype(F32)
+            ext[h][SIDE * chunk + t] = value.astype(BF16)
 
         @pl.when(s < STEPS - 1)
         def _():
@@ -334,20 +374,14 @@
     o = lax.axis_index("obs")
     f = lax.axis_index("flux")
     c = jnp.where(f % 2 == 1, no - 1 - o, o)
-    live = jnp.arange(slots, dtype=jnp.int32) < counts[0, 0]
-    block_obs, block_flux = jac_obs[0, 0], jac_flux[0, 0]
-    own = lax.dynamic_slice_in_dim(neighbours, c * chunk, chunk, 0).reshape(-1)
+    own = lax.dynamic_slice_in_dim(neighbours, c * chunk, chunk, 0).reshape(1, -1)
     own = own - (f * tiles + c * chunk - SIDE * chunk)
-    entry_tile = jnp.arange(chunk * nbrs, dtype=jnp.int32) // nbrs
-    fwd = segment_pairs(jnp.where(live, block_obs, obs_blocks), block_flux, obs_blocks, tiles, fwd_pairs)
-    adj = segment_pairs(jnp.where(live, block_flux, tiles), block_obs, tiles, obs_blocks, adj_pairs)
-    gat = segment_pairs(own, entry_tile, reach, chunk, gat_pairs)
-    idx = jnp.concatenate([fwd, adj, gat, own])
+    own = jnp.pad(own, ((0, 0), (0, LANES - own.shape[1])), constant_values=NOBODY)
+    assert slots % LANES == 0 and slots < 1024 and max(reach, tiles, obs_blocks) < NOBODY
+    assert max(fwd_pairs, adj_pairs) <= 2 * LANES and chunk * nbrs <= LANES
     g = dict(
         no=no, nf=nf, flux_minor=flux_minor, chunk=chunk, tiles=tiles, obs_blocks=obs_blocks, nbrs=nbrs, slots=slots,
         fwd_pairs=fwd_pairs, adj_pairs=adj_pairs, gat_pairs=gat_pairs,
-        fwd_at=0, adj_at=fwd.shape[0], gat_at=fwd.shape[0] + adj.shape[0],
-        nbr_at=fwd.shape[0] + adj.shape[0] + gat.shape[0],
         fwd_unroll=unroll_of(fwd_pairs, 108), adj_unroll=unroll_of(adj_pairs, 108),
         gat_unroll=unroll_of(gat_pairs, 56),
     )
@@ -361,9 +395,16 @@
     return pl.pallas_call(
         functools.partial(kernel, g),
         out_shape=jax.ShapeDtypeStruct((tiles,) + tile, BF16),
-        in_specs=[pl.BlockSpec(memory_space=pltpu.SMEM), any_space, any_space, any_space, vmem],
+        in_specs=[any_space] * 8,
         out_specs=vmem,
         scratch_shapes=[
+            pltpu.SMEM((16, 4 * LANES), jnp.int32),
+            pltpu.VMEM((16, 4 * LANES), jnp.int32),
+            pltpu.VMEM((1, LANES), jnp.int32),
+            pltpu.VMEM((1, 1, slots), jnp.int32),
+            pltpu.VMEM((1, 1, slots), jnp.int32),
+            pltpu.VMEM((1, 1), jnp.int32),
+            pltpu.VMEM((obs_blocks, width), F32),
             pltpu.VMEM((slots, width, width), BF16),
             pltpu.VMEM((slots, width, width), BF16),
             pltpu.VMEM((chunk, nbrs, width, width), BF16),
@@ -379,7 +420,7 @@
             pltpu.VMEM((2, no - 1, chunk) + half, BF16),
             pltpu.VMEM((2, reach) + half, BF16),
             pltpu.VMEM((2, 2 * SIDE, chunk) + half, BF16),
-            dma((4,)),
+            dma((10,)),
             dma((2,)), dma((2,)), dma((2,)), dma((2,)),
             dma((2,)), dma((2,)), dma((2,)), dma((2,)),
             dma((2,)), dma((2,)), dma((2,)), dma((2,)),
@@ -387,7 +428,7 @@
         compiler_params=pltpu.CompilerParams(
             collective_id=0, has_side_effects=True, vmem_limit_bytes=48 * 1024 * 1024
         ),
-    )(idx, probes, prior_tiles, jac[0, 0], rinv)
+    )(own, jac_obs, jac_flux, counts, probes, prior_tiles, jac[0, 0], rinv)
 
 
 def solution(mesh):

time: 159 us -> 156 us (0.981)
  other arithmetic: 4.91 us -> 0.76 us
  Pallas kernels: 149 us -> 151 us
    reduce_sum x18 -> x0, other arithmetic: 2.57 us -> none  [the longest x3 0.68 us: segment_pairs(): jnp.sum(jnp.where(match, lhs[None, :] - zero_lhs, 0), axis=1)]
    unnamed x5 -> x9, local copies, waits for them, and re-layouts: 2.46 us -> 3.82 us
where the time goes in v4:
time: 156 us
  Pallas kernels  151 us (97%)
  local copies, waits for them, and re-layouts  3.99 us (3%)
    pallas_call x1, Pallas kernels, shards(): pl.pallas_call(functools.partial(kernel, g), out_shape=jax.ShapeDtypeStru...  151 us
    unnamed x9, local copies, waits for them, and re-layouts  3.82 us

profile of v4, /device:TPU:1, one launch (start us, length us, event | category | flops | bytes accessed | tf_op | source)
XLA Modules:
  0.0 156.0 jit_solution(6012233864259735099)
XLA Ops:
  0.7 0.8 dynamic-slice_subtract_fusion
  1.4 0.1 copy.9
  1.5 0.1 sub.27
  1.6 0.0 copy-start
  1.6 1.0 copy-done
  2.6 0.0 copy-start.1
  2.6 0.7 copy-done.1
  3.3 0.0 copy-start.2
  3.3 0.7 copy-done.2
  4.0 0.0 copy-start.3
  4.0 0.7 copy-done.3
  4.7 150.5 %shard_map.82 = bf16[48,32,128]{2,1,0:T(8,128)(2,1)S(1)} custom-call(s32[1,128]{1,0:T(1,128)S(1)} %pad.4.near_in, s32[1,1,384]{2,1,0:T(1,128)S(1)} %copy-done.2, s32[1,1,384]{2,1,0:T(1,128)S(1)} %copy-done.3, s32[1,1]{1,0:T(1,128)S(6)} %copy.11.counts_in, bf16[48,32,128]{2,1,0:T(8,128)(2,1)S(1)} %copy-done, bf16[48,8,128,128]{3,2,1,0:T(8,128)(2,1)} %prior.1, ...), custom_call_target="tpu_custom_call" | custom-call | tf_op jit(solution)/shard_map/pallas_call | solution.py:395
  155.2 0.7 copy.12
  (1 shorter events, 0.0 us)
Async XLA Ops:
  1.6 1.0 copy-start
  2.6 0.7 copy-start.1
  3.3 0.7 copy-start.2
  4.0 0.7 copy-start.3

commit v5 on v4

--- a/solution.py
+++ b/solution.py
@@ -79,6 +79,7 @@
     ext, spread = (ext_a, ext_b), (spread_a, spread_b)
     weighted, adjoint = (weighted_a, weighted_b), (adjoint_a, adjoint_b)
     rows = ext_a.shape[1]
+    nbr_bits = nbrs.bit_length() - 1
     o = lax.axis_index("obs")
     f = lax.axis_index("flux")
     chunks = no * nf
@@ -136,18 +137,6 @@
     for partner in partners:
         pl.semaphore_signal(barrier, inc=1, device_id=partner, device_id_type=MESH)
 
-    for copy in load_small:
-        copy.wait()
-    live = iota((1, slots), 1) < jnp.broadcast_to(count[...], (1, slots))
-    by_obs, by_cell = obs_row[0], cell_row[0]
-    segment_pairs(table, 0, jnp.where(live, by_obs, NOBODY), by_cell, tiles, g["fwd_pairs"])
-    segment_pairs(table, 3, jnp.where(live, by_cell, NOBODY), by_obs, obs_blocks, g["adj_pairs"])
-    entry = iota((1, LANES), 1)
-    by_near = jnp.where(entry < chunk * nbrs, near[...], NOBODY)
-    segment_pairs(table, 6, by_near, jnp.minimum(entry // nbrs, chunk - 1), chunk, g["gat_pairs"])
-    table[9:10, :LANES] = near[...]
-    load_index = pltpu.make_async_copy(table, idx, load_sem.at[4])
-    load_index.start()
     pl.semaphore_wait(barrier, len(partners))
 
     zero = jnp.zeros(spread_a.shape[1:], BF16)
@@ -341,6 +330,25 @@
     for h in range(2):
         load_field[h].wait()
         start_all(field_copies(h))
+
+    for copy in load_small:
+        copy.wait()
+    entry = iota((1, LANES), 1)
+    near_row = jnp.zeros((tiles, LANES), jnp.int32)
+    by_tile = near[...].T
+    for k in range(nbrs):
+        here = (iota((tiles, LANES), 0) == c * chunk + (entry >> nbr_bits)) & ((entry & (nbrs - 1)) == k)
+        near_row = near_row + jnp.where(here, jnp.broadcast_to(by_tile[:, k : k + 1], here.shape), 0)
+    near_row = jnp.clip(total(near_row) - (f * tiles + (c - SIDE) * chunk), 0, reach - 1)
+    live = iota((1, slots), 1) < jnp.broadcast_to(count[...], (1, slots))
+    by_obs, by_cell = obs_row[0], cell_row[0]
+    by_near = jnp.where(entry < chunk * nbrs, near_row, NOBODY)
+    segment_pairs(table, 0, jnp.where(live, by_obs, NOBODY), by_cell, tiles, g["fwd_pairs"])
+    segment_pairs(table, 3, jnp.where(live, by_cell, NOBODY), by_obs, obs_blocks, g["adj_pairs"])
+    segment_pairs(table, 6, by_near, jnp.minimum(entry >> nbr_bits, chunk - 1), chunk, g["gat_pairs"])
+    table[9:10, :LANES] = near_row
+    load_index = pltpu.make_async_copy(table, idx, load_sem.at[4])
+    load_index.start()
 
     def step(s, carry):
         for phase in (spread_phase, forward_phase, weight_phase, adjoint_phase, prior_phase, field_phase):
@@ -371,12 +379,7 @@
     fwd_pairs = (slots + obs_blocks) // 2
     adj_pairs = (slots + tiles) // 2
     gat_pairs = (chunk * nbrs + reach) // 2
-    o = lax.axis_index("obs")
-    f = lax.axis_index("flux")
-    c = jnp.where(f % 2 == 1, no - 1 - o, o)
-    own = lax.dynamic_slice_in_dim(neighbours, c * chunk, chunk, 0).reshape(1, -1)
-    own = own - (f * tiles + c * chunk - SIDE * chunk)
-    own = jnp.pad(own, ((0, 0), (0, LANES - own.shape[1])), constant_values=NOBODY)
+    assert nbrs & (nbrs - 1) == 0
     assert slots % LANES == 0 and slots < 1024 and max(reach, tiles, obs_blocks) < NOBODY
     assert max(fwd_pairs, adj_pairs) <= 2 * LANES and chunk * nbrs <= LANES
     g = dict(
@@ -391,16 +394,16 @@
     dma = pltpu.SemaphoreType.DMA
     most = max(fwd_pairs, adj_pairs, gat_pairs) + 1
     vmem = pl.BlockSpec(memory_space=pltpu.VMEM)
-    any_space = pl.BlockSpec(memory_space=pl.ANY)
+    hbm = pl.BlockSpec(memory_space=pltpu.HBM)
     return pl.pallas_call(
         functools.partial(kernel, g),
         out_shape=jax.ShapeDtypeStruct((tiles,) + tile, BF16),
-        in_specs=[any_space] * 8,
+        in_specs=[hbm] * 8,
         out_specs=vmem,
         scratch_shapes=[
             pltpu.SMEM((16, 4 * LANES), jnp.int32),
             pltpu.VMEM((16, 4 * LANES), jnp.int32),
-            pltpu.VMEM((1, LANES), jnp.int32),
+            pltpu.VMEM((nbrs, tiles), jnp.int32),
             pltpu.VMEM((1, 1, slots), jnp.int32),
             pltpu.VMEM((1, 1, slots), jnp.int32),
             pltpu.VMEM((1, 1), jnp.int32),
@@ -426,9 +429,9 @@
             dma((2,)), dma((2,)), dma((2,)), dma((2,)),
         ],
         compiler_params=pltpu.CompilerParams(
-            collective_id=0, has_side_effects=True, vmem_limit_bytes=48 * 1024 * 1024
+            collective_id=0, has_side_effects=True, vmem_limit_bytes=67043328
         ),
-    )(own, jac_obs, jac_flux, counts, probes, prior_tiles, jac[0, 0], rinv)
+    )(neighbours.T, jac_obs, jac_flux, counts, probes, prior_tiles, jac[0, 0], rinv)
 
 
 def solution(mesh):

time: 156 us -> 154 us (0.987)
  local copies, waits for them, and re-layouts: 3.99 us -> 1.77 us
    unnamed x9 -> x1, local copies, waits for them, and re-layouts: 3.82 us -> 1.77 us
where the time goes in v5:
time: 154 us; the launch traced here: 153 us
  Pallas kernels  151 us (98%)
  local copies, waits for them, and re-layouts  1.77 us (1%)
    pallas_call x1, Pallas kernels, shards(): pl.pallas_call(functools.partial(kernel, g), out_shape=jax.ShapeDtypeStru...  151 us

profile of v5, /device:TPU:1, one launch (start us, length us, event | category | flops | bytes accessed | tf_op | source)
XLA Modules:
  0.0 153.5 jit_solution(9916774396586668798)
XLA Ops:
  0.7 151.1 %shard_map.82 = bf16[48,32,128]{2,1,0:T(8,128)(2,1)} custom-call(s32[8,48]{1,0:T(8,128)} %bitcast.3, s32[1,1,384]{2,1,0:T(1,128)} %obs_in.1, s32[1,1,384]{2,1,0:T(1,128)} %cell_in.1, s32[1,1]{1,0:T(1,128)S(6)} %copy.10.counts_in, bf16[48,32,128]{2,1,0:T(8,128)(2,1)} %probes.1, bf16[48,8,128,128]{3,2,1,0:T(8,128)(2,1)} %prior.1, ...), custom_call_target="tpu_custom_call" | custom-call | tf_op jit(solution)/shard_map/pallas_call | solution.py:398
  151.7 1.8 %copy.11 = bf16[48,32,128]{2,1,0:T(8,128)(2,1)} copy(bf16[48,32,128]{2,1,0:T(8,128)(2,1)} %shard_map.82) | data formatting | bytes 786432

commit v6 on v5

--- a/solution.py
+++ b/solution.py
@@ -233,6 +233,17 @@
             for i, d in enumerate(sides)
         ]
 
+    def flip_third(part):
+        many = unroll_of(slots // 3, 8)
+
+        def flip(i, carry):
+            for u in range(many):
+                at = part * (slots // 3) + i * many + u
+                flipped[at] = blocks[at].T
+            return carry
+
+        lax.fori_loop(0, slots // 3 // many, flip, 0)
+
     def spread_phase(h, s):
         every = field_all(h)
         if h == 0:
@@ -257,6 +268,7 @@
                 for e in range(chunk * nbrs):
                     prior_flip[e] = prior_own[e // nbrs, e % nbrs].T
                 load_jac.wait()
+                flip_third(0)
 
         every.wait_recv()
         products(h, 0, g["fwd_pairs"], spread, blocks, g["fwd_unroll"])
@@ -270,14 +282,7 @@
         if h == 0:
             @pl.when(s == 0)
             def _():
-                many = unroll_of(slots, 8)
-
-                def flip(i, carry):
-                    for u in range(many):
-                        flipped[i * many + u] = blocks[i * many + u].T
-                    return carry
-
-                lax.fori_loop(0, slots // many, flip, 0)
+                flip_third(1)
 
         every.wait_recv()
         for b in range(mine):
@@ -290,6 +295,11 @@
 
     def adjoint_phase(h, s):
         every = weighted_all(h)
+        if h == 0:
+            @pl.when(s == 0)
+            def _():
+                flip_third(2)
+
         every.wait_recv()
         products(h, 3, g["adj_pairs"], weighted, flipped, g["adj_unroll"])
         for t in range(tiles):
@@ -380,7 +390,7 @@
     adj_pairs = (slots + tiles) // 2
     gat_pairs = (chunk * nbrs + reach) // 2
     assert nbrs & (nbrs - 1) == 0
-    assert slots % LANES == 0 and slots < 1024 and max(reach, tiles, obs_blocks) < NOBODY
+    assert slots % LANES == 0 and slots % 3 == 0 and slots < 1024 and max(reach, tiles, obs_blocks) < NOBODY
     assert max(fwd_pairs, adj_pairs) <= 2 * LANES and chunk * nbrs <= LANES
     g = dict(
         no=no, nf=nf, flux_minor=flux_minor, chunk=chunk, tiles=tiles, obs_blocks=obs_blocks, nbrs=nbrs, slots=slots,

time: 154 us -> 150 us (0.974)
  Pallas kernels: 151 us -> 148 us
    pallas_call x1, Pallas kernels: 151 us -> 148 us  [shards(): pl.pallas_call(functools.partial(kernel, g), out_shape=jax.ShapeDtypeStru...]
where the time goes in v6:
time: 150 us
  Pallas kernels  148 us (99%)
  local copies, waits for them, and re-layouts  1.77 us (1%)
    pallas_call x1, Pallas kernels, shards(): pl.pallas_call(functools.partial(kernel, g), out_shape=jax.ShapeDtypeStru...  148 us

profile of v6, /device:TPU:1, one launch (start us, length us, event | category | flops | bytes accessed | tf_op | source)
XLA Modules:
  0.0 150.5 jit_solution(6173498056947953902)
XLA Ops:
  0.7 148.0 %shard_map.82 = bf16[48,32,128]{2,1,0:T(8,128)(2,1)} custom-call(s32[8,48]{1,0:T(8,128)} %bitcast.3, s32[1,1,384]{2,1,0:T(1,128)} %obs_in.1, s32[1,1,384]{2,1,0:T(1,128)} %cell_in.1, s32[1,1]{1,0:T(1,128)S(6)} %copy.10.counts_in, bf16[48,32,128]{2,1,0:T(8,128)(2,1)} %probes.1, bf16[48,8,128,128]{3,2,1,0:T(8,128)(2,1)} %prior.1, ...), custom_call_target="tpu_custom_call" | custom-call | tf_op jit(solution)/shard_map/pallas_call | solution.py:408
  148.7 1.8 %copy.11 = bf16[48,32,128]{2,1,0:T(8,128)(2,1)} copy(bf16[48,32,128]{2,1,0:T(8,128)(2,1)} %shard_map.82) | data formatting | bytes 786432

commit v7 on v6

--- a/solution.py
+++ b/solution.py
@@ -404,7 +404,8 @@
     dma = pltpu.SemaphoreType.DMA
     most = max(fwd_pairs, adj_pairs, gat_pairs) + 1
     vmem = pl.BlockSpec(memory_space=pltpu.VMEM)
-    hbm = pl.BlockSpec(memory_space=pltpu.HBM)
+    hbm = pl.BlockSpec(memory_space=pl.ANY)
+    held = functools.partial(pltpu.with_memory_space_constraint, memory_space=pltpu.HBM)
     return pl.pallas_call(
         functools.partial(kernel, g),
         out_shape=jax.ShapeDtypeStruct((tiles,) + tile, BF16),
@@ -439,9 +440,9 @@
             dma((2,)), dma((2,)), dma((2,)), dma((2,)),
         ],
         compiler_params=pltpu.CompilerParams(
-            collective_id=0, has_side_effects=True, vmem_limit_bytes=67043328
+            collective_id=0, has_side_effects=True, vmem_limit_bytes=48 * 1024 * 1024
         ),
-    )(neighbours.T, jac_obs, jac_flux, counts, probes, prior_tiles, jac[0, 0], rinv)
+    )(held(neighbours.T), held(jac_obs), held(jac_flux), counts, held(probes), prior_tiles, jac[0, 0], held(rinv))
 
 
 def solution(mesh):

time: 150 us -> 149 us (level); the launches traced: 150 us -> 148 us
  Pallas kernels: 148 us -> 146 us
    pallas_call x1, Pallas kernels: 148 us -> 146 us  [shards(): pl.pallas_call(functools.partial(kernel, g), out_shape=jax.ShapeDtypeStru...]
where the time goes in v7:
time: 149 us; the launch traced here: 148 us
  Pallas kernels  146 us (98%)
    pallas_call x1, Pallas kernels, shards(): pl.pallas_call(functools.partial(kernel, g), out_shape=jax.ShapeDtypeStru...  146 us

profile of v7, /device:TPU:1, one launch (start us, length us, event | category | flops | bytes accessed | tf_op | source)
XLA Modules:
  0.0 147.9 jit_solution(14157011628620478548)
XLA Ops:
  0.7 146.5 %shard_map.82 = bf16[48,32,128]{2,1,0:T(8,128)(2,1)S(1)} custom-call(s32[8,48]{1,0:T(8,128)} %bitcast.3, s32[1,1,384]{2,1,0:T(1,128)} %obs_in.1, s32[1,1,384]{2,1,0:T(1,128)} %cell_in.1, s32[1,1]{1,0:T(1,128)S(6)} %copy.10.counts_in, bf16[48,32,128]{2,1,0:T(8,128)(2,1)} %probes.1, bf16[48,8,128,128]{3,2,1,0:T(8,128)(2,1)} %prior.1, ...), custom_call_target="tpu_custom_call" | custom-call | tf_op jit(solution)/shard_map/pallas_call | solution.py:409
  147.1 0.7 copy.11
